TPU v7x, 32 devices: a whole 2x2x4 slice. The times are simulated.
32 devices in a mesh: gx: 4 (over z), gy: 2 (over y), gz: 4 (over x, core).
Axes of the slice: x: 2, y: 2, z: 4, core: 2. Of those that a mesh axis runs over, the one named last changes fastest.
Arguments:
- random_vectors: float32 [64, 16, 128, 128], P('gx', 'gy', 'gz'), may hold values from -6 to 6
- potential: float32 [64, 16, 128], P('gx', 'gy', 'gz'), may hold values from -2.5 to 2.5
Outputs:
- moments: float32 [9, 128], replicated
- chebyshev_vector: float32 [64, 16, 128, 128], P('gx', 'gy', 'gz')
All inputs are finite; a program needn't handle non-finite values.
Results may differ from a plain program's by a relative error of at most 0.0001.
Values sent between devices are 32-bit elements; how exact they have to be, the bound alone decides.
No kernel may reach another device: no remote copies, remote signals or barrier semaphores. Data moves between devices by JAX's collectives and lax.ppermute only.
A program may use at most 64 MiB of HBM per device.

v0:
```python
import jax
import jax.numpy as jnp
from jax import lax
from jax.sharding import PartitionSpec as P

ITERS = 4


def extended(cells, sides, width):
    for axis, dim in sides:
        count = lax.axis_size(axis)
        head = lax.slice_in_dim(cells, 0, width, axis=dim)
        tail = lax.slice_in_dim(cells, cells.shape[dim] - width, cells.shape[dim], axis=dim)
        cells = jnp.concatenate(
            [
                lax.ppermute(tail, axis, [(i, (i + 1) % count) for i in range(count)]),
                cells,
                lax.ppermute(head, axis, [((i + 1) % count, i) for i in range(count)]),
            ],
            axis=dim,
        )
    return cells


def local_product(left, right):
    return jnp.sum(left * right, axis=(0, 1, 2))


def shards(random_vectors, potential):
    onsite = potential[..., None]

    def apply_hamiltonian(field):
        along_x = extended(field, (("gx", 0),), 1)
        along_y = extended(field, (("gy", 1),), 1)
        along_z = extended(field, (("gz", 2),), 1)
        beside = along_x[2:] + along_x[:-2]
        beside = beside + along_y[:, 2:] + along_y[:, :-2]
        beside = beside + along_z[:, :, 2:] + along_z[:, :, :-2]
        return (onsite * field - beside) / 9.0

    sites_total = (
        random_vectors.shape[0]
        * lax.axis_size("gx")
        * (random_vectors.shape[1] * lax.axis_size("gy"))
        * (random_vectors.shape[2] * lax.axis_size("gz"))
    )
    highest = 2 * ITERS
    terms = [random_vectors]
    while len(terms) <= highest:
        if len(terms) == 1:
            terms.append(apply_hamiltonian(random_vectors))
        else:
            terms.append(2.0 * apply_hamiltonian(terms[-1]) - terms[-2])
    keep = terms[ITERS]
    sums = [local_product(random_vectors, term) for term in terms]
    totals = lax.psum(jnp.stack(sums), ("gx", "gy", "gz"))
    moments = totals / sites_total
    return (moments, keep)


def solution(mesh):
    in_specs = (P("gx", "gy", "gz", None), P("gx", "gy", "gz"))
    out_specs = (P(), P("gx", "gy", "gz", None))
    return jax.shard_map(shards, mesh=mesh, in_specs=in_specs, out_specs=out_specs, check_vma=False)
```

profile of v0, /device:TPU:0, one launch (start us, length us, event | category | flops | bytes accessed | tf_op | source)
XLA Modules:
  0.0 187.3 jit_solution(8045725559561875424)
XLA Ops:
  1.9 2.5 %collective-permute-start.4 = (f32[16,8,1,128]{3,2,1,0:T(1,128)S(1)}, f32[16,8,1,128]{3,2,1,0:T(1,128)S(1)}, u32[]{:S(2)}, u32[]{:S(2)}) collective-permute-start(f32[16,8,1,128]{3,2,1,0:T(1,128)S(1)} %get-tuple-element.58), channel_id=1, source_target_pairs={{1,0},{2,1},{3,2},{0,3},{5,4},{6,5},{7,6},{4,7},{9,8},{10,9},{11,1... | collective-permute-start | bytes 196616 | tf_op jit(solution)/shard_map/ppermute | solution.py:18
  8.5 3.7 %collective-permute-start = (f32[1,8,32,128]{3,2,1,0:T(8,128)S(1)}, f32[1,8,32,128]{3,2,1,0:T(8,128)S(1)}, u32[]{:S(2)}, u32[]{:S(2)}) collective-permute-start(f32[1,8,32,128]{3,2,1,0:T(8,128)S(1)} %get-tuple-element.54), channel_id=1, source_target_pairs={{8,0},{16,8},{24,16},{0,24},{9,1},{17,9},{25,17},{1,25},{10,2},{18... | collective-permute-start | bytes 393224 | tf_op jit(solution)/shard_map/ppermute | solution.py:18
  12.3 3.7 %collective-permute-done.5 = f32[16,8,1,128]{3,2,1,0:T(1,128)S(1)} collective-permute-done((f32[16,8,1,128]{3,2,1,0:T(1,128)S(1)}, f32[16,8,1,128]{3,2,1,0:T(1,128)S(1)}, u32[]{:S(2)}, u32[]{:S(2)}) %collective-permute-start.5) | collective-permute-done | bytes 65568 | tf_op jit(solution)/shard_map/ppermute | solution.py:16
  16.0 3.0 %collective-permute-done.1 = f32[1,8,32,128]{3,2,1,0:T(8,128)S(1)} collective-permute-done((f32[1,8,32,128]{3,2,1,0:T(8,128)S(1)}, f32[1,8,32,128]{3,2,1,0:T(8,128)S(1)}, u32[]{:S(2)}, u32[]{:S(2)}) %collective-permute-start.1) | collective-permute-done | bytes 131104 | tf_op jit(solution)/shard_map/ppermute | solution.py:16
  19.0 8.5 %broadcast_multiply_fusion = f32[16,8,32,128]{3,2,1,0:T(8,128)S(1)} fusion(f32[16,8,32,128]{3,2,1,0:T(8,128)} %param.2, f32[16,8,1,128]{3,2,1,0:T(1,128)S(1)} %collective-permute-done.5, f32[16,8,1,128]{3,2,1,0:T(1,128)S(1)} %collective-permute-done.4, f32[16,1,32,128]{3,2,1,0:T(8,128)S(1)} %collective-permute-done.3, ...), kind=kLoop, calls=%fused_computation.120 | loop fusion | flops 7340032 | bytes 5128192 | tf_op jit(solution)/shard_map/div | solution.py:39
  30.4 3.7 %collective-permute-start.6 = (f32[1,8,32,128]{3,2,1,0:T(8,128)S(1)}, f32[1,8,32,128]{3,2,1,0:T(8,128)S(1)}, u32[]{:S(2)}, u32[]{:S(2)}) collective-permute-start(f32[1,8,32,128]{3,2,1,0:T(8,128)S(1)} %get-tuple-element.48), channel_id=1, source_target_pairs={{8,0},{16,8},{24,16},{0,24},{9,1},{17,9},{25,17},{1,25},{10,2},{18... | collective-permute-start | bytes 393224 | tf_op jit(solution)/shard_map/ppermute | solution.py:18
  34.1 3.9 %collective-permute-done.6 = f32[1,8,32,128]{3,2,1,0:T(8,128)S(1)} collective-permute-done((f32[1,8,32,128]{3,2,1,0:T(8,128)S(1)}, f32[1,8,32,128]{3,2,1,0:T(8,128)S(1)}, u32[]{:S(2)}, u32[]{:S(2)}) %collective-permute-start.6) | collective-permute-done | bytes 131104 | tf_op jit(solution)/shard_map/ppermute | solution.py:18
  38.0 3.9 %collective-permute-done.7 = f32[1,8,32,128]{3,2,1,0:T(8,128)S(1)} collective-permute-done((f32[1,8,32,128]{3,2,1,0:T(8,128)S(1)}, f32[1,8,32,128]{3,2,1,0:T(8,128)S(1)}, u32[]{:S(2)}, u32[]{:S(2)}) %collective-permute-start.7) | collective-permute-done | bytes 131104 | tf_op jit(solution)/shard_map/ppermute | solution.py:16
  42.0 4.3 %fusion.53 = f32[16,8,32,128]{3,2,1,0:T(8,128)S(1)} fusion(f32[16,8,32,128]{3,2,1,0:T(8,128)S(1)} %copy-done, f32[16,8,32,128]{3,2,1,0:T(8,128)S(1)} %broadcast_multiply_fusion, f32[16,8,1,128]{3,2,1,0:T(1,128)S(1)} %collective-permute-done.11, f32[16,8,1,128]{3,2,1,0:T(1,128)S(1)} %collective-permute-done.10, ...), kind=kLoop, calls=%fused_computation.90 | loop fusion | flops 14680064 | bytes 8159232 | tf_op jit(solution)/shard_map/sub | solution.py:53
  48.9 3.4 %collective-permute-start.12 = (f32[1,8,32,128]{3,2,1,0:T(8,128)S(1)}, f32[1,8,32,128]{3,2,1,0:T(8,128)S(1)}, u32[]{:S(2)}, u32[]{:S(2)}) collective-permute-start(f32[1,8,32,128]{3,2,1,0:T(8,128)S(1)} %get-tuple-element.42), channel_id=1, source_target_pairs={{8,0},{16,8},{24,16},{0,24},{9,1},{17,9},{25,17},{1,25},{10,2},{18... | collective-permute-start | bytes 393224 | tf_op jit(solution)/shard_map/ppermute | solution.py:18
  52.5 3.6 %collective-permute-done.17 = f32[16,8,1,128]{3,2,1,0:T(1,128)S(1)} collective-permute-done((f32[16,8,1,128]{3,2,1,0:T(1,128)S(1)}, f32[16,8,1,128]{3,2,1,0:T(1,128)S(1)}, u32[]{:S(2)}, u32[]{:S(2)}) %collective-permute-start.17) | collective-permute-done | bytes 65568 | tf_op jit(solution)/shard_map/ppermute | solution.py:16
  56.2 3.4 %collective-permute-done.13 = f32[1,8,32,128]{3,2,1,0:T(8,128)S(1)} collective-permute-done((f32[1,8,32,128]{3,2,1,0:T(8,128)S(1)}, f32[1,8,32,128]{3,2,1,0:T(8,128)S(1)}, u32[]{:S(2)}, u32[]{:S(2)}) %collective-permute-start.13) | collective-permute-done | bytes 131104 | tf_op jit(solution)/shard_map/ppermute | solution.py:16
  60.1 4.4 %fusion.45 = f32[16,8,32,128]{3,2,1,0:T(8,128)S(1)} fusion(f32[16,8,32,128]{3,2,1,0:T(8,128)S(1)} %fusion.53, f32[16,8,1,128]{3,2,1,0:T(1,128)S(1)} %collective-permute-done.17, f32[16,8,1,128]{3,2,1,0:T(1,128)S(1)} %collective-permute-done.16, f32[16,1,32,128]{3,2,1,0:T(8,128)S(1)} %collective-permute-done.15, ...), kind=kLoop, calls=%fused_computation.76 | loop fusion | flops 15204352 | bytes 8142848 | tf_op jit(solution)/shard_map/sub | solution.py:53
  66.8 2.8 %collective-permute-start.18 = (f32[1,8,32,128]{3,2,1,0:T(8,128)S(1)}, f32[1,8,32,128]{3,2,1,0:T(8,128)S(1)}, u32[]{:S(2)}, u32[]{:S(2)}) collective-permute-start(f32[1,8,32,128]{3,2,1,0:T(8,128)S(1)} %get-tuple-element.36), channel_id=1, source_target_pairs={{8,0},{16,8},{24,16},{0,24},{9,1},{17,9},{25,17},{1,25},{10,2},{18... | collective-permute-start | bytes 393224 | tf_op jit(solution)/shard_map/ppermute | solution.py:18
  70.7 2.8 %collective-permute-done.23 = f32[16,8,1,128]{3,2,1,0:T(1,128)S(1)} collective-permute-done((f32[16,8,1,128]{3,2,1,0:T(1,128)S(1)}, f32[16,8,1,128]{3,2,1,0:T(1,128)S(1)}, u32[]{:S(2)}, u32[]{:S(2)}) %collective-permute-start.23) | collective-permute-done | bytes 65568 | tf_op jit(solution)/shard_map/ppermute | solution.py:16
  73.6 3.4 %collective-permute-done.19 = f32[1,8,32,128]{3,2,1,0:T(8,128)S(1)} collective-permute-done((f32[1,8,32,128]{3,2,1,0:T(8,128)S(1)}, f32[1,8,32,128]{3,2,1,0:T(8,128)S(1)}, u32[]{:S(2)}, u32[]{:S(2)}) %collective-permute-start.19) | collective-permute-done | bytes 131104 | tf_op jit(solution)/shard_map/ppermute | solution.py:16
  77.4 2.5 %fusion.37 = f32[16,8,32,128]{3,2,1,0:T(8,128)S(1)} fusion(f32[16,8,32,128]{3,2,1,0:T(8,128)S(1)} %fusion.53, f32[16,8,32,128]{3,2,1,0:T(8,128)S(1)} %fusion.45, f32[16,8,1,128]{3,2,1,0:T(1,128)S(1)} %collective-permute-done.23, f32[16,8,1,128]{3,2,1,0:T(1,128)S(1)} %collective-permute-done.22, f32[16,1,32,128]{3,2,1,0:T(8,128)S(1)} %collective-permute-done.21, ...), kind=kLoop, calls=%fused_computation.62 | loop fusion | flops 7864320 | bytes 7225344 | tf_op jit(solution)/shard_map/sub | solution.py:53
  86.3 2.4 %collective-permute-done.29 = f32[16,8,1,128]{3,2,1,0:T(1,128)S(1)} collective-permute-done((f32[16,8,1,128]{3,2,1,0:T(1,128)S(1)}, f32[16,8,1,128]{3,2,1,0:T(1,128)S(1)}, u32[]{:S(2)}, u32[]{:S(2)}) %collective-permute-start.29) | collective-permute-done | bytes 65568 | tf_op jit(solution)/shard_map/ppermute | solution.py:16
  88.8 3.0 %collective-permute-done.25 = f32[1,8,32,128]{3,2,1,0:T(8,128)S(1)} collective-permute-done((f32[1,8,32,128]{3,2,1,0:T(8,128)S(1)}, f32[1,8,32,128]{3,2,1,0:T(8,128)S(1)}, u32[]{:S(2)}, u32[]{:S(2)}) %collective-permute-start.25) | collective-permute-done | bytes 131104 | tf_op jit(solution)/shard_map/ppermute | solution.py:16
  92.9 4.5 %multiply_reduce_fusion.2 = (f32[128]{0:T(128)S(1)}, f32[128]{0:T(128)S(1)}, f32[16,8,32,128]{3,2,1,0:T(8,128)S(1)}) fusion(f32[16,8,32,128]{3,2,1,0:T(8,128)S(1)} %copy-done, f32[16,8,1,128]{3,2,1,0:T(1,128)S(1)} %collective-permute-done.5, f32[16,8,1,128]{3,2,1,0:T(1,128)S(1)} %collective-permute-done.4, ...), kind=kLoop, calls=%fused_computation.114 | loop fusion | flops 17301248 | bytes 10241024 | tf_op jit(solution)/shard_map/reduce_sum | solution.py:26
  101.8 2.4 %collective-permute-start.35 = (f32[16,8,1,128]{3,2,1,0:T(1,128)S(1)}, f32[16,8,1,128]{3,2,1,0:T(1,128)S(1)}, u32[]{:S(2)}, u32[]{:S(2)}) collective-permute-start(f32[16,8,1,128]{3,2,1,0:T(1,128)S(1)} %get-tuple-element.29), channel_id=1, source_target_pairs={{0,1},{1,2},{2,3},{3,0},{4,5},{5,6},{6,7},{7,4},{8,9},{9,10},{10,1... | collective-permute-start | bytes 196616 | tf_op jit(solution)/shard_map/ppermute | solution.py:16
  105.6 3.6 %collective-permute-done.31 = f32[1,8,32,128]{3,2,1,0:T(8,128)S(1)} collective-permute-done((f32[1,8,32,128]{3,2,1,0:T(8,128)S(1)}, f32[1,8,32,128]{3,2,1,0:T(8,128)S(1)}, u32[]{:S(2)}, u32[]{:S(2)}) %collective-permute-start.31) | collective-permute-done | bytes 131104 | tf_op jit(solution)/shard_map/ppermute | solution.py:16
  109.6 2.5 %fusion.21 = f32[16,8,32,128]{3,2,1,0:T(8,128)S(1)} fusion(f32[16,8,32,128]{3,2,1,0:T(8,128)S(1)} %fusion.37, f32[16,8,32,128]{3,2,1,0:T(8,128)S(1)} %get-tuple-element.11, f32[16,8,1,128]{3,2,1,0:T(1,128)S(1)} %collective-permute-done.35, f32[16,8,1,128]{3,2,1,0:T(1,128)S(1)} %collective-permute-done.34, f32[16,1,32,128]{3,2,1,0:T(8,128)S(1)} %collective-permute-done.33, ...), kind=kLoop, calls=%fused_computation.34 | loop fusion | flops 7864320 | bytes 7225344 | tf_op jit(solution)/shard_map/sub | solution.py:53
  114.4 2.2 %collective-permute-start.36 = (f32[1,8,32,128]{3,2,1,0:T(8,128)S(1)}, f32[1,8,32,128]{3,2,1,0:T(8,128)S(1)}, u32[]{:S(2)}, u32[]{:S(2)}) collective-permute-start(f32[1,8,32,128]{3,2,1,0:T(8,128)S(1)} %get-tuple-element.18), channel_id=1, source_target_pairs={{8,0},{16,8},{24,16},{0,24},{9,1},{17,9},{25,17},{1,25},{10,2},{18... | collective-permute-start | bytes 393224 | tf_op jit(solution)/shard_map/ppermute | solution.py:18
  116.6 2.9 %collective-permute-start.41 = (f32[16,8,1,128]{3,2,1,0:T(1,128)S(1)}, f32[16,8,1,128]{3,2,1,0:T(1,128)S(1)}, u32[]{:S(2)}, u32[]{:S(2)}) collective-permute-start(f32[16,8,1,128]{3,2,1,0:T(1,128)S(1)} %get-tuple-element.23), channel_id=1, source_target_pairs={{0,1},{1,2},{2,3},{3,0},{4,5},{5,6},{6,7},{7,4},{8,9},{9,10},{10,1... | collective-permute-start | bytes 196616 | tf_op jit(solution)/shard_map/ppermute | solution.py:16
  120.6 4.8 %collective-permute-done.37 = f32[1,8,32,128]{3,2,1,0:T(8,128)S(1)} collective-permute-done((f32[1,8,32,128]{3,2,1,0:T(8,128)S(1)}, f32[1,8,32,128]{3,2,1,0:T(8,128)S(1)}, u32[]{:S(2)}, u32[]{:S(2)}) %collective-permute-start.37) | collective-permute-done | bytes 131104 | tf_op jit(solution)/shard_map/ppermute | solution.py:16
  125.4 2.5 %fusion.13 = f32[16,8,32,128]{3,2,1,0:T(8,128)S(1)} fusion(f32[16,8,32,128]{3,2,1,0:T(8,128)S(1)} %get-tuple-element.11, f32[16,8,32,128]{3,2,1,0:T(8,128)S(1)} %fusion.21, f32[16,8,1,128]{3,2,1,0:T(1,128)S(1)} %collective-permute-done.41, f32[16,8,1,128]{3,2,1,0:T(1,128)S(1)} %collective-permute-done.40, f32[16,1,32,128]{3,2,1,0:T(8,128)S(1)} %collective-permute-done.39, ...), kind=kLoop, calls=%fused_computation.20 | loop fusion | flops 7864320 | bytes 7225344 | tf_op jit(solution)/shard_map/sub | solution.py:53
  132.3 3.7 %collective-permute-done.47 = f32[16,8,1,128]{3,2,1,0:T(1,128)S(1)} collective-permute-done((f32[16,8,1,128]{3,2,1,0:T(1,128)S(1)}, f32[16,8,1,128]{3,2,1,0:T(1,128)S(1)}, u32[]{:S(2)}, u32[]{:S(2)}) %collective-permute-start.47) | collective-permute-done | bytes 65568 | tf_op jit(solution)/shard_map/ppermute | solution.py:16
  136.2 4.0 %collective-permute-done.43 = f32[1,8,32,128]{3,2,1,0:T(8,128)S(1)} collective-permute-done((f32[1,8,32,128]{3,2,1,0:T(8,128)S(1)}, f32[1,8,32,128]{3,2,1,0:T(8,128)S(1)}, u32[]{:S(2)}, u32[]{:S(2)}) %collective-permute-start.43) | collective-permute-done | bytes 131104 | tf_op jit(solution)/shard_map/ppermute | solution.py:16
  140.2 2.2 %collective-permute-done.45 = f32[16,1,32,128]{3,2,1,0:T(8,128)S(1)} collective-permute-done((f32[16,1,32,128]{3,2,1,0:T(8,128)S(1)}, f32[16,1,32,128]{3,2,1,0:T(8,128)S(1)}, u32[]{:S(2)}, u32[]{:S(2)}) %collective-permute-start.45) | collective-permute-done | bytes 262176 | tf_op jit(solution)/shard_map/ppermute | solution.py:16
  142.4 3.6 %fusion.5 = (f32[128]{0:T(128)S(1)}, f32[128]{0:T(128)S(1)}, f32[128]{0:T(128)S(1)}, f32[128]{0:T(128)S(1)}, f32[128]{0:T(128)S(1)}, /*index=5*/f32[128]{0:T(128)S(1)}, f32[128]{0:T(128)S(1)}) fusion(f32[16,8,32,128]{3,2,1,0:T(8,128)S(1)} %copy-done, f32[16,8,32,128]{3,2,1,0:T(8,128)S(1)} %fusion.21, f32[16,8,32,128]{3,2,1,0:T(8,128)S(1)} %fusion.13, ...), kind=kLoop, calls=%fused_computation.6 | loop fusion | flops 15203456 | bytes 13520384 | tf_op jit(solution)/shard_map/reduce_sum | solution.py:26
  146.1 40.6 %psum.7 = f32[9,128]{1,0:T(8,128)S(1)} all-reduce(f32[9,128]{1,0:T(8,128)S(1)} %stack.39), channel_id=1, replica_groups=mesh['gx'=4,'gy'=2,'gz'=4] {'gx','gy','gz'}, use_global_device_ids=true, to_apply=%region_9.0 | all-reduce | flops 1152 | bytes 9216 | tf_op jit(solution)/shard_map/psum | solution.py:56
  (106 shorter events, 38.2 us)
Async XLA Ops:
  1.9 10.3 %collective-permute-start.4 = (f32[16,8,1,128]{3,2,1,0:T(1,128)S(1)}, f32[16,8,1,128]{3,2,1,0:T(1,128)S(1)}, u32[]{:S(2)}, u32[]{:S(2)}) collective-permute-start(f32[16,8,1,128]{3,2,1,0:T(1,128)S(1)} %get-tuple-element.58), channel_id=1, source_target_pairs={{1,0},{2,1},{3,2},{0,3},{5,4},{6,5},{7,6},{4,7},{9,8},{10,9},{11,1... | collective-permute-start | bytes 196616 | tf_op jit(solution)/shard_map/ppermute | solution.py:18
  5.5 13.5 %collective-permute-start.2 = (f32[16,1,32,128]{3,2,1,0:T(8,128)S(1)}, f32[16,1,32,128]{3,2,1,0:T(8,128)S(1)}, u32[]{:S(2)}, u32[]{:S(2)}) collective-permute-start(f32[16,1,32,128]{3,2,1,0:T(8,128)S(1)} %get-tuple-element.56), channel_id=1, source_target_pairs={{4,0},{0,4},{5,1},{1,5},{6,2},{2,6},{7,3},{3,7},{12,8},{8,12},{13,... | collective-permute-start | bytes 786440 | tf_op jit(solution)/shard_map/ppermute | solution.py:18
  7.1 11.9 %collective-permute-start.3 = (f32[16,1,32,128]{3,2,1,0:T(8,128)S(1)}, f32[16,1,32,128]{3,2,1,0:T(8,128)S(1)}, u32[]{:S(2)}, u32[]{:S(2)}) collective-permute-start(f32[16,1,32,128]{3,2,1,0:T(8,128)S(1)} %get-tuple-element.57), channel_id=1, source_target_pairs={{0,4},{4,0},{1,5},{5,1},{2,6},{6,2},{3,7},{7,3},{8,12},{12,8},{9,1... | collective-permute-start | bytes 786440 | tf_op jit(solution)/shard_map/ppermute | solution.py:16
  8.5 7.4 %collective-permute-start = (f32[1,8,32,128]{3,2,1,0:T(8,128)S(1)}, f32[1,8,32,128]{3,2,1,0:T(8,128)S(1)}, u32[]{:S(2)}, u32[]{:S(2)}) collective-permute-start(f32[1,8,32,128]{3,2,1,0:T(8,128)S(1)} %get-tuple-element.54), channel_id=1, source_target_pairs={{8,0},{16,8},{24,16},{0,24},{9,1},{17,9},{25,17},{1,25},{10,2},{18... | collective-permute-start | bytes 393224 | tf_op jit(solution)/shard_map/ppermute | solution.py:18
  12.2 6.8 %collective-permute-start.1 = (f32[1,8,32,128]{3,2,1,0:T(8,128)S(1)}, f32[1,8,32,128]{3,2,1,0:T(8,128)S(1)}, u32[]{:S(2)}, u32[]{:S(2)}) collective-permute-start(f32[1,8,32,128]{3,2,1,0:T(8,128)S(1)} %get-tuple-element.55), channel_id=1, source_target_pairs={{0,8},{8,16},{16,24},{24,0},{1,9},{9,17},{17,25},{25,1},{2,10},{10... | collective-permute-start | bytes 393224 | tf_op jit(solution)/shard_map/ppermute | solution.py:16
  27.6 6.5 %collective-permute-start.10 = (f32[16,8,1,128]{3,2,1,0:T(1,128)S(1)}, f32[16,8,1,128]{3,2,1,0:T(1,128)S(1)}, u32[]{:S(2)}, u32[]{:S(2)}) collective-permute-start(f32[16,8,1,128]{3,2,1,0:T(1,128)S(1)} %get-tuple-element.52), channel_id=1, source_target_pairs={{1,0},{2,1},{3,2},{0,3},{5,4},{6,5},{7,6},{4,7},{9,8},{10,9},{11,1... | collective-permute-start | bytes 196616 | tf_op jit(solution)/shard_map/ppermute | solution.py:18
  28.3 13.6 %collective-permute-start.8 = (f32[16,1,32,128]{3,2,1,0:T(8,128)S(1)}, f32[16,1,32,128]{3,2,1,0:T(8,128)S(1)}, u32[]{:S(2)}, u32[]{:S(2)}) collective-permute-start(f32[16,1,32,128]{3,2,1,0:T(8,128)S(1)} %get-tuple-element.50), channel_id=1, source_target_pairs={{4,0},{0,4},{5,1},{1,5},{6,2},{2,6},{7,3},{3,7},{12,8},{8,12},{13,... | collective-permute-start | bytes 786440 | tf_op jit(solution)/shard_map/ppermute | solution.py:18
  29.8 12.1 %collective-permute-start.9 = (f32[16,1,32,128]{3,2,1,0:T(8,128)S(1)}, f32[16,1,32,128]{3,2,1,0:T(8,128)S(1)}, u32[]{:S(2)}, u32[]{:S(2)}) collective-permute-start(f32[16,1,32,128]{3,2,1,0:T(8,128)S(1)} %get-tuple-element.51), channel_id=1, source_target_pairs={{0,4},{4,0},{1,5},{5,1},{2,6},{6,2},{3,7},{7,3},{8,12},{12,8},{9,1... | collective-permute-start | bytes 786440 | tf_op jit(solution)/shard_map/ppermute | solution.py:16
  30.4 7.6 %collective-permute-start.6 = (f32[1,8,32,128]{3,2,1,0:T(8,128)S(1)}, f32[1,8,32,128]{3,2,1,0:T(8,128)S(1)}, u32[]{:S(2)}, u32[]{:S(2)}) collective-permute-start(f32[1,8,32,128]{3,2,1,0:T(8,128)S(1)} %get-tuple-element.48), channel_id=1, source_target_pairs={{8,0},{16,8},{24,16},{0,24},{9,1},{17,9},{25,17},{1,25},{10,2},{18... | collective-permute-start | bytes 393224 | tf_op jit(solution)/shard_map/ppermute | solution.py:18
  34.1 7.8 %collective-permute-start.7 = (f32[1,8,32,128]{3,2,1,0:T(8,128)S(1)}, f32[1,8,32,128]{3,2,1,0:T(8,128)S(1)}, u32[]{:S(2)}, u32[]{:S(2)}) collective-permute-start(f32[1,8,32,128]{3,2,1,0:T(8,128)S(1)} %get-tuple-element.49), channel_id=1, source_target_pairs={{0,8},{8,16},{16,24},{24,0},{1,9},{9,17},{17,25},{25,1},{2,10},{10... | collective-permute-start | bytes 393224 | tf_op jit(solution)/shard_map/ppermute | solution.py:16
  46.5 13.2 %collective-permute-start.14 = (f32[16,1,32,128]{3,2,1,0:T(8,128)S(1)}, f32[16,1,32,128]{3,2,1,0:T(8,128)S(1)}, u32[]{:S(2)}, u32[]{:S(2)}) collective-permute-start(f32[16,1,32,128]{3,2,1,0:T(8,128)S(1)} %get-tuple-element.44), channel_id=1, source_target_pairs={{4,0},{0,4},{5,1},{1,5},{6,2},{2,6},{7,3},{3,7},{12,8},{8,12},{13,... | collective-permute-start | bytes 786440 | tf_op jit(solution)/shard_map/ppermute | solution.py:18
  48.1 12.0 %collective-permute-start.15 = (f32[16,1,32,128]{3,2,1,0:T(8,128)S(1)}, f32[16,1,32,128]{3,2,1,0:T(8,128)S(1)}, u32[]{:S(2)}, u32[]{:S(2)}) collective-permute-start(f32[16,1,32,128]{3,2,1,0:T(8,128)S(1)} %get-tuple-element.45), channel_id=1, source_target_pairs={{0,4},{4,0},{1,5},{5,1},{2,6},{6,2},{3,7},{7,3},{8,12},{12,8},{9,1... | collective-permute-start | bytes 786440 | tf_op jit(solution)/shard_map/ppermute | solution.py:16
  48.9 7.3 %collective-permute-start.12 = (f32[1,8,32,128]{3,2,1,0:T(8,128)S(1)}, f32[1,8,32,128]{3,2,1,0:T(8,128)S(1)}, u32[]{:S(2)}, u32[]{:S(2)}) collective-permute-start(f32[1,8,32,128]{3,2,1,0:T(8,128)S(1)} %get-tuple-element.42), channel_id=1, source_target_pairs={{8,0},{16,8},{24,16},{0,24},{9,1},{17,9},{25,17},{1,25},{10,2},{18... | collective-permute-start | bytes 393224 | tf_op jit(solution)/shard_map/ppermute | solution.py:18
  52.3 7.3 %collective-permute-start.13 = (f32[1,8,32,128]{3,2,1,0:T(8,128)S(1)}, f32[1,8,32,128]{3,2,1,0:T(8,128)S(1)}, u32[]{:S(2)}, u32[]{:S(2)}) collective-permute-start(f32[1,8,32,128]{3,2,1,0:T(8,128)S(1)} %get-tuple-element.43), channel_id=1, source_target_pairs={{0,8},{8,16},{16,24},{24,0},{1,9},{9,17},{17,25},{25,1},{2,10},{10... | collective-permute-start | bytes 393224 | tf_op jit(solution)/shard_map/ppermute | solution.py:16
  64.7 12.4 %collective-permute-start.20 = (f32[16,1,32,128]{3,2,1,0:T(8,128)S(1)}, f32[16,1,32,128]{3,2,1,0:T(8,128)S(1)}, u32[]{:S(2)}, u32[]{:S(2)}) collective-permute-start(f32[16,1,32,128]{3,2,1,0:T(8,128)S(1)} %get-tuple-element.38), channel_id=1, source_target_pairs={{4,0},{0,4},{5,1},{1,5},{6,2},{2,6},{7,3},{3,7},{12,8},{8,12},{13,... | collective-permute-start | bytes 786440 | tf_op jit(solution)/shard_map/ppermute | solution.py:18
  66.2 11.2 %collective-permute-start.21 = (f32[16,1,32,128]{3,2,1,0:T(8,128)S(1)}, f32[16,1,32,128]{3,2,1,0:T(8,128)S(1)}, u32[]{:S(2)}, u32[]{:S(2)}) collective-permute-start(f32[16,1,32,128]{3,2,1,0:T(8,128)S(1)} %get-tuple-element.39), channel_id=1, source_target_pairs={{0,4},{4,0},{1,5},{5,1},{2,6},{6,2},{3,7},{7,3},{8,12},{12,8},{9,1... | collective-permute-start | bytes 786440 | tf_op jit(solution)/shard_map/ppermute | solution.py:16
  66.8 6.7 %collective-permute-start.18 = (f32[1,8,32,128]{3,2,1,0:T(8,128)S(1)}, f32[1,8,32,128]{3,2,1,0:T(8,128)S(1)}, u32[]{:S(2)}, u32[]{:S(2)}) collective-permute-start(f32[1,8,32,128]{3,2,1,0:T(8,128)S(1)} %get-tuple-element.36), channel_id=1, source_target_pairs={{8,0},{16,8},{24,16},{0,24},{9,1},{17,9},{25,17},{1,25},{10,2},{18... | collective-permute-start | bytes 393224 | tf_op jit(solution)/shard_map/ppermute | solution.py:18
  69.6 7.4 %collective-permute-start.19 = (f32[1,8,32,128]{3,2,1,0:T(8,128)S(1)}, f32[1,8,32,128]{3,2,1,0:T(8,128)S(1)}, u32[]{:S(2)}, u32[]{:S(2)}) collective-permute-start(f32[1,8,32,128]{3,2,1,0:T(8,128)S(1)} %get-tuple-element.37), channel_id=1, source_target_pairs={{0,8},{8,16},{16,24},{24,0},{1,9},{9,17},{17,25},{25,1},{2,10},{10... | collective-permute-start | bytes 393224 | tf_op jit(solution)/shard_map/ppermute | solution.py:16
  80.1 11.7 %collective-permute-start.26 = (f32[16,1,32,128]{3,2,1,0:T(8,128)S(1)}, f32[16,1,32,128]{3,2,1,0:T(8,128)S(1)}, u32[]{:S(2)}, u32[]{:S(2)}) collective-permute-start(f32[16,1,32,128]{3,2,1,0:T(8,128)S(1)} %get-tuple-element.32), channel_id=1, source_target_pairs={{4,0},{0,4},{5,1},{1,5},{6,2},{2,6},{7,3},{3,7},{12,8},{8,12},{13,... | collective-permute-start | bytes 786440 | tf_op jit(solution)/shard_map/ppermute | solution.py:18
  81.6 11.2 %collective-permute-start.27 = (f32[16,1,32,128]{3,2,1,0:T(8,128)S(1)}, f32[16,1,32,128]{3,2,1,0:T(8,128)S(1)}, u32[]{:S(2)}, u32[]{:S(2)}) collective-permute-start(f32[16,1,32,128]{3,2,1,0:T(8,128)S(1)} %get-tuple-element.33), channel_id=1, source_target_pairs={{0,4},{4,0},{1,5},{5,1},{2,6},{6,2},{3,7},{7,3},{8,12},{12,8},{9,1... | collective-permute-start | bytes 786440 | tf_op jit(solution)/shard_map/ppermute | solution.py:16
  82.3 6.4 %collective-permute-start.24 = (f32[1,8,32,128]{3,2,1,0:T(8,128)S(1)}, f32[1,8,32,128]{3,2,1,0:T(8,128)S(1)}, u32[]{:S(2)}, u32[]{:S(2)}) collective-permute-start(f32[1,8,32,128]{3,2,1,0:T(8,128)S(1)} %get-tuple-element.30), channel_id=1, source_target_pairs={{8,0},{16,8},{24,16},{0,24},{9,1},{17,9},{25,17},{1,25},{10,2},{18... | collective-permute-start | bytes 393224 | tf_op jit(solution)/shard_map/ppermute | solution.py:18
  84.3 7.5 %collective-permute-start.25 = (f32[1,8,32,128]{3,2,1,0:T(8,128)S(1)}, f32[1,8,32,128]{3,2,1,0:T(8,128)S(1)}, u32[]{:S(2)}, u32[]{:S(2)}) collective-permute-start(f32[1,8,32,128]{3,2,1,0:T(8,128)S(1)} %get-tuple-element.31), channel_id=1, source_target_pairs={{0,8},{8,16},{16,24},{24,0},{1,9},{9,17},{17,25},{25,1},{2,10},{10... | collective-permute-start | bytes 393224 | tf_op jit(solution)/shard_map/ppermute | solution.py:16
  97.5 11.8 %collective-permute-start.32 = (f32[16,1,32,128]{3,2,1,0:T(8,128)S(1)}, f32[16,1,32,128]{3,2,1,0:T(8,128)S(1)}, u32[]{:S(2)}, u32[]{:S(2)}) collective-permute-start(f32[16,1,32,128]{3,2,1,0:T(8,128)S(1)} %get-tuple-element.26), channel_id=1, source_target_pairs={{4,0},{0,4},{5,1},{1,5},{6,2},{2,6},{7,3},{3,7},{12,8},{8,12},{13,... | collective-permute-start | bytes 786440 | tf_op jit(solution)/shard_map/ppermute | solution.py:18
  99.1 10.4 %collective-permute-start.33 = (f32[16,1,32,128]{3,2,1,0:T(8,128)S(1)}, f32[16,1,32,128]{3,2,1,0:T(8,128)S(1)}, u32[]{:S(2)}, u32[]{:S(2)}) collective-permute-start(f32[16,1,32,128]{3,2,1,0:T(8,128)S(1)} %get-tuple-element.27), channel_id=1, source_target_pairs={{0,4},{4,0},{1,5},{5,1},{2,6},{6,2},{3,7},{7,3},{8,12},{12,8},{9,1... | collective-permute-start | bytes 786440 | tf_op jit(solution)/shard_map/ppermute | solution.py:16
  101.0 8.3 %collective-permute-start.31 = (f32[1,8,32,128]{3,2,1,0:T(8,128)S(1)}, f32[1,8,32,128]{3,2,1,0:T(8,128)S(1)}, u32[]{:S(2)}, u32[]{:S(2)}) collective-permute-start(f32[1,8,32,128]{3,2,1,0:T(8,128)S(1)} %get-tuple-element.25), channel_id=1, source_target_pairs={{0,8},{8,16},{16,24},{24,0},{1,9},{9,17},{17,25},{25,1},{2,10},{10... | collective-permute-start | bytes 393224 | tf_op jit(solution)/shard_map/ppermute | solution.py:16
  112.2 13.2 %collective-permute-start.38 = (f32[16,1,32,128]{3,2,1,0:T(8,128)S(1)}, f32[16,1,32,128]{3,2,1,0:T(8,128)S(1)}, u32[]{:S(2)}, u32[]{:S(2)}) collective-permute-start(f32[16,1,32,128]{3,2,1,0:T(8,128)S(1)} %get-tuple-element.20), channel_id=1, source_target_pairs={{4,0},{0,4},{5,1},{1,5},{6,2},{2,6},{7,3},{3,7},{12,8},{8,12},{13,... | collective-permute-start | bytes 786440 | tf_op jit(solution)/shard_map/ppermute | solution.py:18
  113.8 11.6 %collective-permute-start.39 = (f32[16,1,32,128]{3,2,1,0:T(8,128)S(1)}, f32[16,1,32,128]{3,2,1,0:T(8,128)S(1)}, u32[]{:S(2)}, u32[]{:S(2)}) collective-permute-start(f32[16,1,32,128]{3,2,1,0:T(8,128)S(1)} %get-tuple-element.21), channel_id=1, source_target_pairs={{0,4},{4,0},{1,5},{5,1},{2,6},{6,2},{3,7},{7,3},{8,12},{12,8},{9,1... | collective-permute-start | bytes 786440 | tf_op jit(solution)/shard_map/ppermute | solution.py:16
  114.4 6.3 %collective-permute-start.36 = (f32[1,8,32,128]{3,2,1,0:T(8,128)S(1)}, f32[1,8,32,128]{3,2,1,0:T(8,128)S(1)}, u32[]{:S(2)}, u32[]{:S(2)}) collective-permute-start(f32[1,8,32,128]{3,2,1,0:T(8,128)S(1)} %get-tuple-element.18), channel_id=1, source_target_pairs={{8,0},{16,8},{24,16},{0,24},{9,1},{17,9},{25,17},{1,25},{10,2},{18... | collective-permute-start | bytes 393224 | tf_op jit(solution)/shard_map/ppermute | solution.py:18
  116.6 8.8 %collective-permute-start.37 = (f32[1,8,32,128]{3,2,1,0:T(8,128)S(1)}, f32[1,8,32,128]{3,2,1,0:T(8,128)S(1)}, u32[]{:S(2)}, u32[]{:S(2)}) collective-permute-start(f32[1,8,32,128]{3,2,1,0:T(8,128)S(1)} %get-tuple-element.19), channel_id=1, source_target_pairs={{0,8},{8,16},{16,24},{24,0},{1,9},{9,17},{17,25},{25,1},{2,10},{10... | collective-permute-start | bytes 393224 | tf_op jit(solution)/shard_map/ppermute | solution.py:16
  128.1 12.1 %collective-permute-start.44 = (f32[16,1,32,128]{3,2,1,0:T(8,128)S(1)}, f32[16,1,32,128]{3,2,1,0:T(8,128)S(1)}, u32[]{:S(2)}, u32[]{:S(2)}) collective-permute-start(f32[16,1,32,128]{3,2,1,0:T(8,128)S(1)} %get-tuple-element.14), channel_id=1, source_target_pairs={{4,0},{0,4},{5,1},{1,5},{6,2},{2,6},{7,3},{3,7},{12,8},{8,12},{13,... | collective-permute-start | bytes 786440 | tf_op jit(solution)/shard_map/ppermute | solution.py:18
  129.7 12.7 %collective-permute-start.45 = (f32[16,1,32,128]{3,2,1,0:T(8,128)S(1)}, f32[16,1,32,128]{3,2,1,0:T(8,128)S(1)}, u32[]{:S(2)}, u32[]{:S(2)}) collective-permute-start(f32[16,1,32,128]{3,2,1,0:T(8,128)S(1)} %get-tuple-element.15), channel_id=1, source_target_pairs={{0,4},{4,0},{1,5},{5,1},{2,6},{6,2},{3,7},{7,3},{8,12},{12,8},{9,1... | collective-permute-start | bytes 786440 | tf_op jit(solution)/shard_map/ppermute | solution.py:16
  132.3 7.9 %collective-permute-start.43 = (f32[1,8,32,128]{3,2,1,0:T(8,128)S(1)}, f32[1,8,32,128]{3,2,1,0:T(8,128)S(1)}, u32[]{:S(2)}, u32[]{:S(2)}) collective-permute-start(f32[1,8,32,128]{3,2,1,0:T(8,128)S(1)} %get-tuple-element.13), channel_id=1, source_target_pairs={{0,8},{8,16},{16,24},{24,0},{1,9},{9,17},{17,25},{25,1},{2,10},{10... | collective-permute-start | bytes 393224 | tf_op jit(solution)/shard_map/ppermute | solution.py:16
  (19 other events, 167.9 us)
where the time goes:
time: 188 us; the launch traced here: 187 us
  waiting for transfers between devices  56.8 us (30%)
  starting transfers between devices  51.1 us (27%)
  blocking collectives  40.6 us (22%)
  other arithmetic  33.4 us (18%)
  local copies, waits for them, and re-layouts  4.45 us (2%)
    ppermute x24, waiting for transfers between devices, extended(): lax.ppermute(tail, axis, [(i, (i + 1) % count) for i in range(count)])  52.4 us
    psum x1, blocking collectives, shards(): totals = lax.psum(jnp.stack(sums), ('gx', 'gy', 'gz'))  40.6 us
    ppermute x24, starting transfers between devices, extended(): lax.ppermute(head, axis, [((i + 1) % count, i) for i in range(count)])  37.6 us
    sub x5, other arithmetic, shards(): terms.append(2.0 * apply_hamiltonian(terms[-1]) - terms[-2])  16.2 us
    ppermute x24, starting transfers between devices, extended(): lax.ppermute(tail, axis, [(i, (i + 1) % count) for i in range(count)])  13.5 us
    div x1, other arithmetic, apply_hamiltonian(): return (onsite * field - beside) / 9.0  8.46 us
    reduce_sum x2, other arithmetic, local_product(): return jnp.sum(left * right, axis=(0, 1, 2))  8.14 us
    ppermute x24, waiting for transfers between devices, extended(): lax.ppermute(head, axis, [((i + 1) % count, i) for i in range(count)])  4.44 us
  transfers between devices with their start and end apart: 48, of which 25 were waited for; matrix products, arithmetic and copies ran while one was open for 1% of the time, Pallas kernels for 0%

commit v1 on v0

v1 whole, which is shorter than its diff:
```python
import jax
import jax.numpy as jnp
from jax import lax
from jax.sharding import PartitionSpec as P

ITERS = 4


def around(cells, axis, dim):
    count = lax.axis_size(axis)
    size = cells.shape[dim]
    head = lax.slice_in_dim(cells, 0, 1, axis=dim)
    tail = lax.slice_in_dim(cells, size - 1, size, axis=dim)
    if count == 1:
        return tail, head
    if count == 2:
        both = lax.ppermute(jnp.concatenate([tail, head], axis=dim), axis, [(0, 1), (1, 0)])
        return lax.slice_in_dim(both, 0, 1, axis=dim), lax.slice_in_dim(both, 1, 2, axis=dim)
    before = lax.ppermute(tail, axis, [(i, (i + 1) % count) for i in range(count)])
    after = lax.ppermute(head, axis, [((i + 1) % count, i) for i in range(count)])
    return before, after


def neighbours(cells, before, after, dim):
    size = cells.shape[dim]
    down = jnp.concatenate([before, lax.slice_in_dim(cells, 0, size - 1, axis=dim)], axis=dim)
    up = jnp.concatenate([lax.slice_in_dim(cells, 1, size, axis=dim), after], axis=dim)
    return down + up


def sum_everywhere(partial, axes):
    count = 1
    for axis in axes:
        count *= lax.axis_size(axis)
    copies = jnp.broadcast_to(partial[None], (count,) + partial.shape)
    return jnp.sum(lax.all_to_all(copies, axes, 0, 0), axis=0)


def product(left, right):
    return jnp.sum(left * right, axis=(0, 1, 2))


def shards(random_vectors, potential):
    onsite = potential[..., None]

    def apply_hamiltonian(field):
        y = around(field, "gy", 1)
        z = around(field, "gz", 2)
        x = around(field, "gx", 0)
        beside = neighbours(field, *x, 0) + neighbours(field, *y, 1) + neighbours(field, *z, 2)
        return (onsite * field - beside) / 9.0

    axes = ("gx", "gy", "gz")
    sites = random_vectors.shape[0] * random_vectors.shape[1] * random_vectors.shape[2]
    for axis in axes:
        sites *= lax.axis_size(axis)
    terms = [random_vectors, apply_hamiltonian(random_vectors)]
    for _ in range(ITERS - 1):
        terms.append(2.0 * apply_hamiltonian(terms[-1]) - terms[-2])
    sums = [product(terms[n // 2], terms[(n + 1) // 2]) for n in range(2 * ITERS + 1)]
    totals = sum_everywhere(jnp.stack(sums), axes)
    moments = [totals[0], totals[1]]
    for n in range(2, 2 * ITERS + 1):
        moments.append(2.0 * totals[n] - totals[n % 2])
    return (jnp.stack(moments) / sites, terms[ITERS])


def solution(mesh):
    in_specs = (P("gx", "gy", "gz", None), P("gx", "gy", "gz"))
    out_specs = (P(), P("gx", "gy", "gz", None))
    return jax.shard_map(shards, mesh=mesh, in_specs=in_specs, out_specs=out_specs, check_vma=False)
```

time: 188 us -> 99.6 us (0.53)
  blocking collectives: 40.6 us -> 13.9 us
  starting transfers between devices: 51.1 us -> 24.7 us
  other arithmetic: 33.4 us -> 11.8 us
  waiting for transfers between devices: 56.8 us -> 36.8 us
  local copies, waits for them, and re-layouts: 4.45 us -> 11.1 us
    psum x1 -> x0, blocking collectives: 40.6 us -> none  [shards(): totals = lax.psum(jnp.stack(sums), ('gx', 'gy', 'gz'))]
    ppermute x48 -> x20, starting transfers between devices: 51.1 us -> 24.7 us  [the longest x8 14 us: around(): lax.ppermute(head, axis, [((i + 1) % count, i) for i in range(count)])]
    ppermute x48 -> x20, waiting for transfers between devices: 56.8 us -> 36.8 us  [the longest x4 36.8 us: around(): lax.ppermute(jnp.concatenate([tail, head], axis=dim), axis, [(0, 1), (1,...]
    all_to_all x0 -> x1, blocking collectives: none -> 13.9 us  [sum_everywhere(): return jnp.sum(lax.all_to_all(copies, axes, 0, 0), axis=0)]
    sub x5 -> x2, other arithmetic: 16.2 us -> 4.71 us  [shards(): terms.append(2.0 * apply_hamiltonian(terms[-1]) - terms[-2])]
    div x1, other arithmetic: 8.46 us -> 2.22 us  [apply_hamiltonian(): return (onsite * field - beside) / 9.0]
    slice x24 -> x29, local copies, waits for them, and re-layouts: 4.39 us -> 10.5 us  [the longest x8 3.72 us: around(): tail = lax.slice_in_dim(cells, size - 1, size, axis=dim)]
    reduce_sum x2, other arithmetic: 8.14 us -> 4.08 us  [the longest x1 4.04 us: product(): return jnp.sum(left * right, axis=(0, 1, 2))]
  transfers between devices with their start and end apart: 48 -> 20, of which waited for: 25 -> 4; matrix products, arithmetic and copies ran while one was open for 1% -> 6% of each run, Pallas kernels for 0% -> 0%
where the time goes in v1:
time: 99.6 us; the launch traced here: 99.4 us
  waiting for transfers between devices  36.8 us (37%)
  starting transfers between devices  24.7 us (25%)
  blocking collectives  13.9 us (14%)
  other arithmetic  11.8 us (12%)
  local copies, waits for them, and re-layouts  11.1 us (11%)
  between operations  1.04 us (1%)
    ppermute x4, waiting for transfers between devices, around(): lax.ppermute(jnp.concatenate([tail, head], axis=dim), axis, [(0, 1), (1,...  36.8 us
    ppermute x8, starting transfers between devices, around(): lax.ppermute(head, axis, [((i + 1) % count, i) for i in range(count)])  14 us
    all_to_all x1, blocking collectives, sum_everywhere(): return jnp.sum(lax.all_to_all(copies, axes, 0, 0), axis=0)  13.9 us
    ppermute x4, starting transfers between devices, around(): lax.ppermute(jnp.concatenate([tail, head], axis=dim), axis, [(0, 1), (1,...  6.49 us
    sub x2, other arithmetic, shards(): terms.append(2.0 * apply_hamiltonian(terms[-1]) - terms[-2])  4.71 us
    ppermute x8, starting transfers between devices, around(): lax.ppermute(tail, axis, [(i, (i + 1) % count) for i in range(count)])  4.23 us
    reduce_sum x1, other arithmetic, product(): return jnp.sum(left * right, axis=(0, 1, 2))  4.04 us
    slice x8, local copies, waits for them, and re-layouts, around(): tail = lax.slice_in_dim(cells, size - 1, size, axis=dim)  3.72 us
  transfers between devices with their start and end apart: 20, of which 4 were waited for; matrix products, arithmetic and copies ran while one was open for 6% of the time, Pallas kernels for 0%

profile of v1, /device:TPU:0, one launch (start us, length us, event | category | flops | bytes accessed | tf_op | source)
XLA Modules:
  0.0 99.4 jit_solution(6031063590546542347)
XLA Ops:
  0.6 1.5 %fusion.49 = (f32[16,8,1,128]{3,2,1,0:T(1,128)S(1)}, f32[16,8,1,128]{3,2,1,0:T(1,128)S(1)}) fusion(f32[16,8,32,128]{3,2,1,0:T(8,128)} %param.2), kind=kLoop, calls=%fused_computation.82 | loop fusion | bytes 262144 | tf_op jit(solution)/shard_map/slice | solution.py:13
  2.1 0.5 collective-permute-start.3
  2.6 2.0 %collective-permute-start.4 = (f32[16,8,1,128]{3,2,1,0:T(1,128)S(1)}, f32[16,8,1,128]{3,2,1,0:T(1,128)S(1)}, u32[]{:S(2)}, u32[]{:S(2)}) collective-permute-start(f32[16,8,1,128]{3,2,1,0:T(1,128)S(1)} %get-tuple-element.59), channel_id=1, source_target_pairs={{1,0},{2,1},{3,2},{0,3},{5,4},{6,5},{7,6},{4,7},{9,8},{10,9},{11,1... | collective-permute-start | bytes 196616 | tf_op jit(solution)/shard_map/ppermute | solution.py:20
  4.6 1.0 fusion.45
  5.6 2.4 %collective-permute-start = (f32[1,8,32,128]{3,2,1,0:T(8,128)S(1)}, f32[1,8,32,128]{3,2,1,0:T(8,128)S(1)}, u32[]{:S(2)}, u32[]{:S(2)}) collective-permute-start(f32[1,8,32,128]{3,2,1,0:T(8,128)S(1)} %get-tuple-element.50), channel_id=1, source_target_pairs={{0,8},{8,16},{16,24},{24,0},{1,9},{9,17},{17,25},{25,1},{2,10},{10... | collective-permute-start | bytes 393224 | tf_op jit(solution)/shard_map/ppermute | solution.py:19
  8.0 2.1 %collective-permute-start.1 = (f32[1,8,32,128]{3,2,1,0:T(8,128)S(1)}, f32[1,8,32,128]{3,2,1,0:T(8,128)S(1)}, u32[]{:S(2)}, u32[]{:S(2)}) collective-permute-start(f32[1,8,32,128]{3,2,1,0:T(8,128)S(1)} %get-tuple-element.51), channel_id=1, source_target_pairs={{8,0},{16,8},{24,16},{0,24},{9,1},{17,9},{25,17},{1,25},{10,2},{18... | collective-permute-start | bytes 393224 | tf_op jit(solution)/shard_map/ppermute | solution.py:20
  10.1 1.1 %fusion.48 = (f32[16,1,32,128]{3,2,1,0:T(8,128)S(1)}, f32[16,1,32,128]{3,2,1,0:T(8,128)S(1)}) fusion(f32[16,8,32,128]{3,2,1,0:T(8,128)} %param.2), kind=kLoop, calls=%fused_computation.81 | loop fusion | bytes 1048576 | tf_op jit(solution)/shard_map/slice | solution.py:13
  11.2 1.7 %collective-permute-start.2 = (f32[16,2,32,128]{3,2,1,0:T(8,128)S(1)}, f32[16,2,32,128]{3,2,1,0:T(8,128)S(1)}, u32[]{:S(2)}, u32[]{:S(2)}) collective-permute-start(f32[16,2,32,128]{3,2,1,0:T(8,128)S(1)} %pad_maximum_fusion), channel_id=1, source_target_pairs={{0,4},{4,0},{1,5},{5,1},{2,6},{6,2},{3,7},{7,3},{8,12},{12,8},{9,1... | collective-permute-start | bytes 1572872 | tf_op jit(solution)/shard_map/ppermute | solution.py:17
  14.8 9.8 %collective-permute-done.2 = f32[16,2,32,128]{3,2,1,0:T(8,128)S(1)} collective-permute-done((f32[16,2,32,128]{3,2,1,0:T(8,128)S(1)}, f32[16,2,32,128]{3,2,1,0:T(8,128)S(1)}, u32[]{:S(2)}, u32[]{:S(2)}) %collective-permute-start.2) | collective-permute-done | bytes 524320 | tf_op jit(solution)/shard_map/ppermute | solution.py:17
  24.8 2.2 %broadcast_multiply_fusion = (f32[16,8,32,128]{3,2,1,0:T(8,128)S(1)}, f32[16,8,32,128]{3,2,1,0:T(8,128)S(1)}) fusion(f32[16,8,1,128]{3,2,1,0:T(1,128)S(1)} %collective-permute-done.4, f32[16,8,31,128]{3,2,1,0:T(8,128)S(1)} %get-tuple-element.61, f32[16,8,31,128]{3,2,1,0:T(8,128)S(1)} %get-tuple-element.60, f32[16,8,1,128]{3,2,1,0:T(1,128)S(1)} %collective-permute-done.3, ...), kind=kLoop, calls=%fused_computation.39 | loop fusion | flops 7340032 | bytes 18890752 | tf_op jit(solution)/shard_map/div | solution.py:51
  28.7 1.6 %collective-permute-start.7 = (f32[16,2,32,128]{3,2,1,0:T(8,128)S(1)}, f32[16,2,32,128]{3,2,1,0:T(8,128)S(1)}, u32[]{:S(2)}, u32[]{:S(2)}) collective-permute-start(f32[16,2,32,128]{3,2,1,0:T(8,128)S(1)} %pad_maximum_fusion.1), channel_id=1, source_target_pairs={{0,4},{4,0},{1,5},{5,1},{2,6},{6,2},{3,7},{7,3},{8,12},{12,8},{9,1... | collective-permute-start | bytes 1572872 | tf_op jit(solution)/shard_map/ppermute | solution.py:17
  30.3 1.7 %collective-permute-start.6 = (f32[1,8,32,128]{3,2,1,0:T(8,128)S(1)}, f32[1,8,32,128]{3,2,1,0:T(8,128)S(1)}, u32[]{:S(2)}, u32[]{:S(2)}) collective-permute-start(f32[1,8,32,128]{3,2,1,0:T(8,128)S(1)} %get-tuple-element.48), channel_id=1, source_target_pairs={{8,0},{16,8},{24,16},{0,24},{9,1},{17,9},{25,17},{1,25},{10,2},{18... | collective-permute-start | bytes 393224 | tf_op jit(solution)/shard_map/ppermute | solution.py:20
  32.9 9.9 %collective-permute-done.7 = f32[16,2,32,128]{3,2,1,0:T(8,128)S(1)} collective-permute-done((f32[16,2,32,128]{3,2,1,0:T(8,128)S(1)}, f32[16,2,32,128]{3,2,1,0:T(8,128)S(1)}, u32[]{:S(2)}, u32[]{:S(2)}) %collective-permute-start.7) | collective-permute-done | bytes 524320 | tf_op jit(solution)/shard_map/ppermute | solution.py:17
  42.9 2.3 %fusion.7 = f32[16,8,32,128]{3,2,1,0:T(8,128)S(1)} fusion(f32[16,8,32,128]{3,2,1,0:T(8,128)S(1)} %copy-done, f32[15,8,32,128]{3,2,1,0:T(8,128)S(1)} %get-tuple-element.47, f32[1,8,32,128]{3,2,1,0:T(8,128)S(1)} %collective-permute-done.5, f32[1,8,32,128]{3,2,1,0:T(8,128)S(1)} %collective-permute-done.6, f32[15,8,32,128]{3,2,1,0:T(8,128)S(1)} %get-tuple-element.46, ...), kind=kLoop, calls=%fused_computation.11 | loop fusion | flops 7864320 | bytes 18890752 | tf_op jit(solution)/shard_map/sub | solution.py:59
  45.3 0.5 fusion.35
  45.9 0.6 fusion.37
  46.5 0.9 collective-permute-start.14
  47.4 1.6 %collective-permute-start.12 = (f32[16,2,32,128]{3,2,1,0:T(8,128)S(1)}, f32[16,2,32,128]{3,2,1,0:T(8,128)S(1)}, u32[]{:S(2)}, u32[]{:S(2)}) collective-permute-start(f32[16,2,32,128]{3,2,1,0:T(8,128)S(1)} %pad_maximum_fusion.2), channel_id=1, source_target_pairs={{0,4},{4,0},{1,5},{5,1},{2,6},{6,2},{3,7},{7,3},{8,12},{12,8},{9,1... | collective-permute-start | bytes 1572872 | tf_op jit(solution)/shard_map/ppermute | solution.py:17
  49.0 1.7 %collective-permute-start.11 = (f32[1,8,32,128]{3,2,1,0:T(8,128)S(1)}, f32[1,8,32,128]{3,2,1,0:T(8,128)S(1)}, u32[]{:S(2)}, u32[]{:S(2)}) collective-permute-start(f32[1,8,32,128]{3,2,1,0:T(8,128)S(1)} %get-tuple-element.36), channel_id=1, source_target_pairs={{8,0},{16,8},{24,16},{0,24},{9,1},{17,9},{25,17},{1,25},{10,2},{18... | collective-permute-start | bytes 393224 | tf_op jit(solution)/shard_map/ppermute | solution.py:20
  51.1 0.5 fusion.33
  51.6 10.1 %collective-permute-done.12 = f32[16,2,32,128]{3,2,1,0:T(8,128)S(1)} collective-permute-done((f32[16,2,32,128]{3,2,1,0:T(8,128)S(1)}, f32[16,2,32,128]{3,2,1,0:T(8,128)S(1)}, u32[]{:S(2)}, u32[]{:S(2)}) %collective-permute-start.12) | collective-permute-done | bytes 524320 | tf_op jit(solution)/shard_map/ppermute | solution.py:17
  61.8 2.4 %fusion.12 = f32[16,8,32,128]{3,2,1,0:T(8,128)S(1)} fusion(f32[15,8,32,128]{3,2,1,0:T(8,128)S(1)} %get-tuple-element.35, f32[1,8,32,128]{3,2,1,0:T(8,128)S(1)} %collective-permute-done.10, f32[1,8,32,128]{3,2,1,0:T(8,128)S(1)} %collective-permute-done.11, f32[15,8,32,128]{3,2,1,0:T(8,128)S(1)} %get-tuple-element.34, ...), kind=kLoop, calls=%fused_computation.19 | loop fusion | flops 8388608 | bytes 18890752 | tf_op jit(solution)/shard_map/sub | solution.py:59
  64.4 0.5 fusion.29
  64.9 0.6 fusion.28
  65.6 1.7 %collective-permute-start.19 = (f32[16,8,1,128]{3,2,1,0:T(1,128)S(1)}, f32[16,8,1,128]{3,2,1,0:T(1,128)S(1)}, u32[]{:S(2)}, u32[]{:S(2)}) collective-permute-start(f32[16,8,1,128]{3,2,1,0:T(1,128)S(1)} %get-tuple-element.23), channel_id=1, source_target_pairs={{1,0},{2,1},{3,2},{0,3},{5,4},{6,5},{7,6},{4,7},{9,8},{10,9},{11,1... | collective-permute-start | bytes 196616 | tf_op jit(solution)/shard_map/ppermute | solution.py:20
  67.4 1.6 %collective-permute-start.17 = (f32[16,2,32,128]{3,2,1,0:T(8,128)S(1)}, f32[16,2,32,128]{3,2,1,0:T(8,128)S(1)}, u32[]{:S(2)}, u32[]{:S(2)}) collective-permute-start(f32[16,2,32,128]{3,2,1,0:T(8,128)S(1)} %pad_maximum_fusion.3), channel_id=1, source_target_pairs={{0,4},{4,0},{1,5},{5,1},{2,6},{6,2},{3,7},{7,3},{8,12},{12,8},{9,1... | collective-permute-start | bytes 1572872 | tf_op jit(solution)/shard_map/ppermute | solution.py:17
  69.1 3.8 %collective-permute-start.16 = (f32[1,8,32,128]{3,2,1,0:T(8,128)S(1)}, f32[1,8,32,128]{3,2,1,0:T(8,128)S(1)}, u32[]{:S(2)}, u32[]{:S(2)}) collective-permute-start(f32[1,8,32,128]{3,2,1,0:T(8,128)S(1)} %get-tuple-element.15), channel_id=1, source_target_pairs={{8,0},{16,8},{24,16},{0,24},{9,1},{17,9},{25,17},{1,25},{10,2},{18... | collective-permute-start | bytes 393224 | tf_op jit(solution)/shard_map/ppermute | solution.py:20
  72.9 0.8 fusion.32
  73.6 6.9 %collective-permute-done.17 = f32[16,2,32,128]{3,2,1,0:T(8,128)S(1)} collective-permute-done((f32[16,2,32,128]{3,2,1,0:T(8,128)S(1)}, f32[16,2,32,128]{3,2,1,0:T(8,128)S(1)}, u32[]{:S(2)}, u32[]{:S(2)}) %collective-permute-start.17) | collective-permute-done | bytes 524320 | tf_op jit(solution)/shard_map/ppermute | solution.py:17
  80.6 4.0 %multiply_reduce_fusion = (f32[128]{0:T(128)S(1)}, f32[128]{0:T(128)S(1)}, f32[128]{0:T(128)S(1)}, f32[128]{0:T(128)S(1)}, f32[128]{0:T(128)S(1)}, /*index=5*/f3...) fusion(f32[16,8,32,128]{3,2,1,0:T(8,128)S(1)} %fusion.12, ...), kind=kLoop, calls=%fused_computation.30 | loop fusion | flops 17824640 | bytes 23089664 | tf_op jit(solution)/shard_map/reduce_sum | solution.py:40
  84.8 13.9 %all_to_all.5 = f32[32,9,128]{2,1,0:T(8,128)S(1)} all-to-all(f32[32,9,128]{2,1,0:T(8,128)S(1)} %broadcast_in_dim.2), channel_id=1, replica_groups=mesh['gx'=4,'gy'=2,'gz'=4] {'gx','gy','gz'}, dimensions={0} | all-to-all | bytes 294912 | tf_op jit(solution)/shard_map/all_to_all | solution.py:36
  98.8 0.6 broadcast_multiply_fusion.2
  (57 shorter events, 5.6 us)
Async XLA Ops:
  0.6 12.3 %copy-start = (f32[16,8,32,128]{3,2,1,0:T(8,128)S(1)}, f32[16,8,32,128]{3,2,1,0:T(8,128)}, u32[]{:S(2)}) copy-start(f32[16,8,32,128]{3,2,1,0:T(8,128)} %param.2) | copy-start | bytes 6291460
  2.1 22.6 %collective-permute-start.3 = (f32[16,8,1,128]{3,2,1,0:T(1,128)S(1)}, f32[16,8,1,128]{3,2,1,0:T(1,128)S(1)}, u32[]{:S(2)}, u32[]{:S(2)}) collective-permute-start(f32[16,8,1,128]{3,2,1,0:T(1,128)S(1)} %get-tuple-element.58), channel_id=1, source_target_pairs={{0,1},{1,2},{2,3},{3,0},{4,5},{5,6},{6,7},{7,4},{8,9},{9,10},{10,1... | collective-permute-start | bytes 196616 | tf_op jit(solution)/shard_map/ppermute | solution.py:19
  2.6 22.1 %collective-permute-start.4 = (f32[16,8,1,128]{3,2,1,0:T(1,128)S(1)}, f32[16,8,1,128]{3,2,1,0:T(1,128)S(1)}, u32[]{:S(2)}, u32[]{:S(2)}) collective-permute-start(f32[16,8,1,128]{3,2,1,0:T(1,128)S(1)} %get-tuple-element.59), channel_id=1, source_target_pairs={{1,0},{2,1},{3,2},{0,3},{5,4},{6,5},{7,6},{4,7},{9,8},{10,9},{11,1... | collective-permute-start | bytes 196616 | tf_op jit(solution)/shard_map/ppermute | solution.py:20
  5.6 19.1 %collective-permute-start = (f32[1,8,32,128]{3,2,1,0:T(8,128)S(1)}, f32[1,8,32,128]{3,2,1,0:T(8,128)S(1)}, u32[]{:S(2)}, u32[]{:S(2)}) collective-permute-start(f32[1,8,32,128]{3,2,1,0:T(8,128)S(1)} %get-tuple-element.50), channel_id=1, source_target_pairs={{0,8},{8,16},{16,24},{24,0},{1,9},{9,17},{17,25},{25,1},{2,10},{10... | collective-permute-start | bytes 393224 | tf_op jit(solution)/shard_map/ppermute | solution.py:19
  8.0 16.8 %collective-permute-start.1 = (f32[1,8,32,128]{3,2,1,0:T(8,128)S(1)}, f32[1,8,32,128]{3,2,1,0:T(8,128)S(1)}, u32[]{:S(2)}, u32[]{:S(2)}) collective-permute-start(f32[1,8,32,128]{3,2,1,0:T(8,128)S(1)} %get-tuple-element.51), channel_id=1, source_target_pairs={{8,0},{16,8},{24,16},{0,24},{9,1},{17,9},{25,17},{1,25},{10,2},{18... | collective-permute-start | bytes 393224 | tf_op jit(solution)/shard_map/ppermute | solution.py:20
  11.2 13.5 %collective-permute-start.2 = (f32[16,2,32,128]{3,2,1,0:T(8,128)S(1)}, f32[16,2,32,128]{3,2,1,0:T(8,128)S(1)}, u32[]{:S(2)}, u32[]{:S(2)}) collective-permute-start(f32[16,2,32,128]{3,2,1,0:T(8,128)S(1)} %pad_maximum_fusion), channel_id=1, source_target_pairs={{0,4},{4,0},{1,5},{5,1},{2,6},{6,2},{3,7},{7,3},{8,12},{12,8},{9,1... | collective-permute-start | bytes 1572872 | tf_op jit(solution)/shard_map/ppermute | solution.py:17
  13.5 0.8 copy-start.1
  28.1 14.7 %collective-permute-start.9 = (f32[16,8,1,128]{3,2,1,0:T(1,128)S(1)}, f32[16,8,1,128]{3,2,1,0:T(1,128)S(1)}, u32[]{:S(2)}, u32[]{:S(2)}) collective-permute-start(f32[16,8,1,128]{3,2,1,0:T(1,128)S(1)} %get-tuple-element.40), channel_id=1, source_target_pairs={{1,0},{2,1},{3,2},{0,3},{5,4},{6,5},{7,6},{4,7},{9,8},{10,9},{11,1... | collective-permute-start | bytes 196616 | tf_op jit(solution)/shard_map/ppermute | solution.py:20
  28.2 14.7 %collective-permute-start.8 = (f32[16,8,1,128]{3,2,1,0:T(1,128)S(1)}, f32[16,8,1,128]{3,2,1,0:T(1,128)S(1)}, u32[]{:S(2)}, u32[]{:S(2)}) collective-permute-start(f32[16,8,1,128]{3,2,1,0:T(1,128)S(1)} %get-tuple-element.41), channel_id=1, source_target_pairs={{0,1},{1,2},{2,3},{3,0},{4,5},{5,6},{6,7},{7,4},{8,9},{9,10},{10,1... | collective-permute-start | bytes 196616 | tf_op jit(solution)/shard_map/ppermute | solution.py:19
  28.7 14.1 %collective-permute-start.7 = (f32[16,2,32,128]{3,2,1,0:T(8,128)S(1)}, f32[16,2,32,128]{3,2,1,0:T(8,128)S(1)}, u32[]{:S(2)}, u32[]{:S(2)}) collective-permute-start(f32[16,2,32,128]{3,2,1,0:T(8,128)S(1)} %pad_maximum_fusion.1), channel_id=1, source_target_pairs={{0,4},{4,0},{1,5},{5,1},{2,6},{6,2},{3,7},{7,3},{8,12},{12,8},{9,1... | collective-permute-start | bytes 1572872 | tf_op jit(solution)/shard_map/ppermute | solution.py:17
  30.3 12.6 %collective-permute-start.6 = (f32[1,8,32,128]{3,2,1,0:T(8,128)S(1)}, f32[1,8,32,128]{3,2,1,0:T(8,128)S(1)}, u32[]{:S(2)}, u32[]{:S(2)}) collective-permute-start(f32[1,8,32,128]{3,2,1,0:T(8,128)S(1)} %get-tuple-element.48), channel_id=1, source_target_pairs={{8,0},{16,8},{24,16},{0,24},{9,1},{17,9},{25,17},{1,25},{10,2},{18... | collective-permute-start | bytes 393224 | tf_op jit(solution)/shard_map/ppermute | solution.py:20
  32.0 10.8 %collective-permute-start.5 = (f32[1,8,32,128]{3,2,1,0:T(8,128)S(1)}, f32[1,8,32,128]{3,2,1,0:T(8,128)S(1)}, u32[]{:S(2)}, u32[]{:S(2)}) collective-permute-start(f32[1,8,32,128]{3,2,1,0:T(8,128)S(1)} %get-tuple-element.49), channel_id=1, source_target_pairs={{0,8},{8,16},{16,24},{24,0},{1,9},{9,17},{17,25},{25,1},{2,10},{10... | collective-permute-start | bytes 393224 | tf_op jit(solution)/shard_map/ppermute | solution.py:19
  46.5 15.3 %collective-permute-start.14 = (f32[16,8,1,128]{3,2,1,0:T(1,128)S(1)}, f32[16,8,1,128]{3,2,1,0:T(1,128)S(1)}, u32[]{:S(2)}, u32[]{:S(2)}) collective-permute-start(f32[16,8,1,128]{3,2,1,0:T(1,128)S(1)} %get-tuple-element.28), channel_id=1, source_target_pairs={{1,0},{2,1},{3,2},{0,3},{5,4},{6,5},{7,6},{4,7},{9,8},{10,9},{11,1... | collective-permute-start | bytes 196616 | tf_op jit(solution)/shard_map/ppermute | solution.py:20
  47.4 14.4 %collective-permute-start.13 = (f32[16,8,1,128]{3,2,1,0:T(1,128)S(1)}, f32[16,8,1,128]{3,2,1,0:T(1,128)S(1)}, u32[]{:S(2)}, u32[]{:S(2)}) collective-permute-start(f32[16,8,1,128]{3,2,1,0:T(1,128)S(1)} %get-tuple-element.29), channel_id=1, source_target_pairs={{0,1},{1,2},{2,3},{3,0},{4,5},{5,6},{6,7},{7,4},{8,9},{9,10},{10,1... | collective-permute-start | bytes 196616 | tf_op jit(solution)/shard_map/ppermute | solution.py:19
  47.4 14.4 %collective-permute-start.12 = (f32[16,2,32,128]{3,2,1,0:T(8,128)S(1)}, f32[16,2,32,128]{3,2,1,0:T(8,128)S(1)}, u32[]{:S(2)}, u32[]{:S(2)}) collective-permute-start(f32[16,2,32,128]{3,2,1,0:T(8,128)S(1)} %pad_maximum_fusion.2), channel_id=1, source_target_pairs={{0,4},{4,0},{1,5},{5,1},{2,6},{6,2},{3,7},{7,3},{8,12},{12,8},{9,1... | collective-permute-start | bytes 1572872 | tf_op jit(solution)/shard_map/ppermute | solution.py:17
  49.0 12.8 %collective-permute-start.11 = (f32[1,8,32,128]{3,2,1,0:T(8,128)S(1)}, f32[1,8,32,128]{3,2,1,0:T(8,128)S(1)}, u32[]{:S(2)}, u32[]{:S(2)}) collective-permute-start(f32[1,8,32,128]{3,2,1,0:T(8,128)S(1)} %get-tuple-element.36), channel_id=1, source_target_pairs={{8,0},{16,8},{24,16},{0,24},{9,1},{17,9},{25,17},{1,25},{10,2},{18... | collective-permute-start | bytes 393224 | tf_op jit(solution)/shard_map/ppermute | solution.py:20
  50.7 11.1 %collective-permute-start.10 = (f32[1,8,32,128]{3,2,1,0:T(8,128)S(1)}, f32[1,8,32,128]{3,2,1,0:T(8,128)S(1)}, u32[]{:S(2)}, u32[]{:S(2)}) collective-permute-start(f32[1,8,32,128]{3,2,1,0:T(8,128)S(1)} %get-tuple-element.37), channel_id=1, source_target_pairs={{0,8},{8,16},{16,24},{24,0},{1,9},{9,17},{17,25},{25,1},{2,10},{10... | collective-permute-start | bytes 393224 | tf_op jit(solution)/shard_map/ppermute | solution.py:19
  65.5 15.1 %collective-permute-start.18 = (f32[16,8,1,128]{3,2,1,0:T(1,128)S(1)}, f32[16,8,1,128]{3,2,1,0:T(1,128)S(1)}, u32[]{:S(2)}, u32[]{:S(2)}) collective-permute-start(f32[16,8,1,128]{3,2,1,0:T(1,128)S(1)} %get-tuple-element.22), channel_id=1, source_target_pairs={{0,1},{1,2},{2,3},{3,0},{4,5},{5,6},{6,7},{7,4},{8,9},{9,10},{10,1... | collective-permute-start | bytes 196616 | tf_op jit(solution)/shard_map/ppermute | solution.py:19
  65.6 15.0 %collective-permute-start.19 = (f32[16,8,1,128]{3,2,1,0:T(1,128)S(1)}, f32[16,8,1,128]{3,2,1,0:T(1,128)S(1)}, u32[]{:S(2)}, u32[]{:S(2)}) collective-permute-start(f32[16,8,1,128]{3,2,1,0:T(1,128)S(1)} %get-tuple-element.23), channel_id=1, source_target_pairs={{1,0},{2,1},{3,2},{0,3},{5,4},{6,5},{7,6},{4,7},{9,8},{10,9},{11,1... | collective-permute-start | bytes 196616 | tf_op jit(solution)/shard_map/ppermute | solution.py:20
  67.4 13.2 %collective-permute-start.17 = (f32[16,2,32,128]{3,2,1,0:T(8,128)S(1)}, f32[16,2,32,128]{3,2,1,0:T(8,128)S(1)}, u32[]{:S(2)}, u32[]{:S(2)}) collective-permute-start(f32[16,2,32,128]{3,2,1,0:T(8,128)S(1)} %pad_maximum_fusion.3), channel_id=1, source_target_pairs={{0,4},{4,0},{1,5},{5,1},{2,6},{6,2},{3,7},{7,3},{8,12},{12,8},{9,1... | collective-permute-start | bytes 1572872 | tf_op jit(solution)/shard_map/ppermute | solution.py:17
  69.0 11.6 %collective-permute-start.15 = (f32[1,8,32,128]{3,2,1,0:T(8,128)S(1)}, f32[1,8,32,128]{3,2,1,0:T(8,128)S(1)}, u32[]{:S(2)}, u32[]{:S(2)}) collective-permute-start(f32[1,8,32,128]{3,2,1,0:T(8,128)S(1)} %get-tuple-element.14), channel_id=1, source_target_pairs={{0,8},{8,16},{16,24},{24,0},{1,9},{9,17},{17,25},{25,1},{2,10},{10... | collective-permute-start | bytes 393224 | tf_op jit(solution)/shard_map/ppermute | solution.py:19
  69.1 11.6 %collective-permute-start.16 = (f32[1,8,32,128]{3,2,1,0:T(8,128)S(1)}, f32[1,8,32,128]{3,2,1,0:T(8,128)S(1)}, u32[]{:S(2)}, u32[]{:S(2)}) collective-permute-start(f32[1,8,32,128]{3,2,1,0:T(8,128)S(1)} %get-tuple-element.15), channel_id=1, source_target_pairs={{8,0},{16,8},{24,16},{0,24},{9,1},{17,9},{25,17},{1,25},{10,2},{18... | collective-permute-start | bytes 393224 | tf_op jit(solution)/shard_map/ppermute | solution.py:20

commit v2 on v1

v2 whole, which is shorter than its diff:
```python
import functools

import jax
import jax.numpy as jnp
from jax import lax
from jax.experimental import pallas as pl
from jax.experimental.pallas import tpu as pltpu
from jax.sharding import PartitionSpec as P


ITERS = 4
AXES = ("gx", "gy", "gz")
TILE = 8
LANES = 128
HALF = LANES // 2


def around(cells, axis, dim):
    count = lax.axis_size(axis)
    size = cells.shape[dim]
    head = lax.slice_in_dim(cells, 0, 1, axis=dim)
    tail = lax.slice_in_dim(cells, size - 1, size, axis=dim)
    if count == 1:
        return tail, head
    if count == 2:
        both = lax.ppermute(jnp.concatenate([tail, head], axis=dim), axis, [(0, 1), (1, 0)])
        return lax.slice_in_dim(both, 0, 1, axis=dim), lax.slice_in_dim(both, 1, 2, axis=dim)
    return to_next(tail, axis), to_previous(head, axis)


def neighbours(cells, before, after, dim):
    size = cells.shape[dim]
    down = jnp.concatenate([before, lax.slice_in_dim(cells, 0, size - 1, axis=dim)], axis=dim)
    up = jnp.concatenate([lax.slice_in_dim(cells, 1, size, axis=dim), after], axis=dim)
    return down + up


def to_next(block, axis):
    count = lax.axis_size(axis)
    return lax.ppermute(block, axis, [(i, (i + 1) % count) for i in range(count)])


def to_previous(block, axis):
    count = lax.axis_size(axis)
    return lax.ppermute(block, axis, [((i + 1) % count, i) for i in range(count)])


def swap(block):
    return lax.ppermute(block, "gy", [(0, 1), (1, 0)])


def sum_over(partial, axes):
    count = 1
    for axis in axes:
        count *= lax.axis_size(axis)
    copies = jnp.broadcast_to(partial[None], (count,) + partial.shape)
    return jnp.sum(lax.all_to_all(copies, axes, 0, 0), axis=0)


def moments_of(totals, shape):
    sites = shape[0] * shape[1] * shape[2]
    for axis in AXES:
        sites *= lax.axis_size(axis)
    lower = jnp.where(jnp.arange(totals.shape[0])[:, None] % 2 == 0, totals[0], totals[1])
    first = jnp.arange(totals.shape[0])[:, None] < 2
    return jnp.where(first, totals, 2.0 * totals - lower) / sites


def step_by_step(random_vectors, potential):
    onsite = potential[..., None]

    def apply_hamiltonian(field):
        y = around(field, "gy", 1)
        z = around(field, "gz", 2)
        x = around(field, "gx", 0)
        beside = neighbours(field, *x, 0) + neighbours(field, *y, 1) + neighbours(field, *z, 2)
        return (onsite * field - beside) / 9.0

    terms = [random_vectors, apply_hamiltonian(random_vectors)]
    for _ in range(ITERS - 1):
        terms.append(2.0 * apply_hamiltonian(terms[-1]) - terms[-2])
    sums = [jnp.sum(terms[n // 2] * terms[(n + 1) // 2], axis=(0, 1, 2)) for n in range(2 * ITERS + 1)]
    return moments_of(sum_over(jnp.stack(sums), AXES), random_vectors.shape), terms[ITERS]


VM = pl.BlockSpec(memory_space=pltpu.VMEM)
SM = pl.BlockSpec(memory_space=pltpu.SMEM)


def call(body, outs, scratch=(), n_in=0, cost=0, limit=8):
    run = pl.pallas_call(
        body,
        out_shape=outs,
        in_specs=[SM] + [VM] * n_in,
        out_specs=jax.tree.map(lambda out: VM if isinstance(out, type(f32(1))) else pl.BlockSpec(memory_space=pl.ANY), outs),
        scratch_shapes=list(scratch),
        cost_estimate=pl.CostEstimate(flops=cost, bytes_accessed=cost, transcendentals=0),
        compiler_params=pltpu.CompilerParams(vmem_limit_bytes=limit * 1024 * 1024),
    )

    def held(place, *blocks):
        return run(place, *(pltpu.with_memory_space_constraint(block, pltpu.VMEM) for block in blocks))

    return held


def f32(*shape):
    return pltpu.VMEM(shape, jnp.float32)


def other_half(place):
    lane = lax.broadcasted_iota(jnp.int32, (TILE, LANES), 1)
    return (lane >= HALF) != (place == 1)


def tile_rows(place, pair, tiles, kept):
    mirror = tiles - 1 - 2 * pair
    which = (1 - place) if kept else place
    return pl.ds(pl.multiple_of((pair + which * mirror) * TILE, TILE), TILE)


def rolled(tile):
    return pltpu.roll(tile, HALF, axis=tile.ndim - 1)


def pack_tile(place, other, src, x, y, pair, tiles):
    kept = src[x, y, tile_rows(place, pair, tiles, True), :]
    moved = src[x, y, tile_rows(place, pair, tiles, False), :]
    return jnp.where(other, kept, rolled(moved))


def merge_tiles(place, other, pay, own, own_x, x, y, slot, pair, tiles, write):
    got = pay[x, y, slot * TILE : (slot + 1) * TILE, :]
    kept = tile_rows(place, pair, tiles, True)
    moved = tile_rows(place, pair, tiles, False)
    write(kept, jnp.where(other, got, own[own_x, y, kept, :]))
    write(moved, jnp.where(other, rolled(got), own[own_x, y, moved, :]))


def pack_kernel(pairs, tiles, place_ref, src, *outs):
    place = place_ref[0]
    other = other_half(place)

    @pl.loop(0, src.shape[0])
    def _(x):
        for y in range(src.shape[1]):
            for out, which in zip(outs, pairs):
                for slot, pair in enumerate(which):
                    out[x, y, slot * TILE : (slot + 1) * TILE, :] = pack_tile(place, other, src, x, y, pair, tiles)


def face_kernel(tiles, place_ref, own, pay, out, z_next, z_previous):
    place = place_ref[0]
    other = other_half(place)

    @pl.loop(0, out.shape[0])
    def _(x):
        for y in range(out.shape[1]):
            for pair in range(tiles // 2):

                def write(rows, tile, y=y):
                    out[x, y, rows, :] = tile

                merge_tiles(place, other, pay, own, x, x, y, pair, pair, tiles, write)
        low = lax.broadcasted_iota(jnp.int32, (TILE, LANES), 0) < TILE // 2
        half = out.shape[1] // 2
        for y in range(half):
            head = [out[x, w, 0:TILE, :] for w in (y, y + half)]
            tail = [out[x, w, (tiles - 1) * TILE : tiles * TILE, :] for w in (y, y + half)]
            z_previous[x, y] = jnp.where(low, head[0], pltpu.roll(head[1], TILE // 2, axis=0))
            z_next[x, y] = jnp.where(low, pltpu.roll(tail[0], TILE // 2, axis=0), tail[1])


def ends_kernel(tiles, place_ref, own, pay, z_next, z_previous):
    place = place_ref[0]
    other = other_half(place)
    half = own.shape[1] // 2

    @pl.loop(0, z_next.shape[0])
    def _(x):
        low = lax.broadcasted_iota(jnp.int32, (TILE, LANES), 0) < TILE // 2

        def end_tiles(y):
            got = pay[x, y]
            turned = rolled(got)
            head_got = jnp.where(place == 1, got, turned)
            tail_got = jnp.where(place == 1, turned, got)
            head = jnp.where(other, head_got, own[x, y, 0:TILE, :])
            tail = jnp.where(other, tail_got, own[x, y, (tiles - 1) * TILE : tiles * TILE, :])
            return head, tail

        for y in range(half):
            a, b = end_tiles(y), end_tiles(y + half)
            z_previous[x, y] = jnp.where(low, a[0], pltpu.roll(b[0], TILE // 2, axis=0))
            z_next[x, y] = jnp.where(low, pltpu.roll(a[1], TILE // 2, axis=0), b[1])


def halo_tiles(low, above, below, x, y):
    up, down = above[x, y], below[x, y]
    return (
        jnp.where(low, up, pltpu.roll(down, TILE // 2, axis=0)),
        jnp.where(low, pltpu.roll(up, TILE // 2, axis=0), down),
    )


def halo_kernel(place_ref, above, below, out):
    half = above.shape[1]

    @pl.loop(0, out.shape[0])
    def _(x):
        low = lax.broadcasted_iota(jnp.int32, (TILE, LANES), 0) < TILE // 2
        for y in range(half):
            out[x, y], out[x, y + half] = halo_tiles(low, above, below, x, y)


def fold(value):
    total = value[0:TILE]
    for start in range(TILE, value.shape[0], TILE):
        total = total + value[start : start + TILE]
    return total


def sweep(level, lo, hi, cur, prev, onsite, out, own_rows, sums=None):
    width = out[0].shape[2]
    rows = out[0].shape[1]

    def row(x, carry):
        carry = list(carry)
        here = [None] * rows

        def at(y):
            if here[y] is None:
                here[y] = cur[0][cur[1] + x, y]
            return here[y]

        for y in range(rows):
            center = at(y)
            below = at(y - 1) if y > 0 else rolled(at(rows - 1))
            above = at(y + 1) if y < rows - 1 else rolled(at(0))
            beside = cur[0][cur[1] + x - 1, y] + cur[0][cur[1] + x + 1, y]
            beside = beside + below + above
            length = center.shape[0]
            beside = beside + pltpu.roll(center, 1, axis=0) + pltpu.roll(center, length - 1, axis=0)
            scaled = onsite[0][onsite[1] + x, y] * center - beside
            if level == 1:
                new = scaled * (1.0 / 9.0)
            else:
                new = scaled * (2.0 / 9.0) - prev[0][prev[1] + x, y]
            new = new[0:width]
            out[0][out[1] + x, y] = new
            if sums is not None:
                mine, base = new[0:own_rows], center[0:own_rows]
                if level == 1:
                    carry[0] = carry[0] + fold(base * base)
                carry[-2] = carry[-2] + fold(base * mine)
                carry[-1] = carry[-1] + fold(mine * mine)
        return tuple(carry)

    if sums is None:
        lax.fori_loop(lo, hi, lambda x, c: row(x, ()) or c, 0)
        return
    count = 3 if level == 1 else 2
    zero = jnp.zeros((TILE, LANES), jnp.float32)
    done = lax.fori_loop(lo, hi, row, (zero,) * count)
    for k, value in enumerate(done):
        sums[2 * level - count + 1 + k] += value


def pack_rows(place, other, src, out):
    tiles = src.shape[2] // TILE

    @pl.loop(0, src.shape[0])
    def _(x):
        for y in range(src.shape[1]):
            for pair in range(tiles // 2):
                out[x, y, pair * TILE : (pair + 1) * TILE, :] = pack_tile(place, other, src, x, y, pair, tiles)


def middle_kernel(n_x, deep, tiles, place_ref, own, pay_ends, pay_rest, left, right, halo_left, halo_right, above, below,
                  onsite, t_out, pay_out, edge1, edge2, edge3, sums, t0, t1, t2, t3):
    place = place_ref[0]
    other = other_half(place)
    z = tiles * TILE
    ny = own.shape[1]

    @pl.loop(0, deep)
    def _(x):
        for y in range(ny):
            t0[x, y, 0:z, :] = left[x, y]
            t0[x, y, z : z + TILE, :] = halo_left[x, y]
            t0[n_x - deep + x, y, 0:z, :] = right[x, y]
            t0[n_x - deep + x, y, z : z + TILE, :] = halo_right[x, y]

    @pl.loop(0, n_x - 2 * deep)
    def _(x):
        low = lax.broadcasted_iota(jnp.int32, (TILE, LANES), 0) < TILE // 2
        for y in range(ny):

            def write(rows, tile, y=y):
                t0[deep + x, y, rows, :] = tile

            merge_tiles(place, other, pay_ends, own, x, x, y, 0, 0, tiles, write)
            for pair in range(1, tiles // 2):
                merge_tiles(place, other, pay_rest, own, x, x, y, pair - 1, pair, tiles, write)
        for y in range(ny // 2):
            first, second = halo_tiles(low, above, below, x, y)
            t0[deep + x, y, z : z + TILE, :] = first
            t0[deep + x, y + ny // 2, z : z + TILE, :] = second

    sums[...] = jnp.zeros_like(sums)
    v = (onsite, 0)
    sweep(1, 1, n_x - 1, (t0, 0), None, v, (t1, 0), z, sums)
    sweep(2, 2, n_x - 2, (t1, 0), (t0, 0), v, (t2, 0), z, sums)
    sweep(3, 3, n_x - 3, (t2, 0), (t1, 0), v, (t3, 0), z, sums)
    sweep(4, 4, n_x - 4, (t3, 0), (t2, 0), v, (t_out, -4), z, sums)
    pack_rows(place, other, t_out, pay_out)
    for edge, ref, low_x in ((edge1, t1, 1), (edge2, t2, 2), (edge3, t3, 3)):
        for k, x in enumerate((low_x, low_x + 1, n_x - 2 - low_x, n_x - 1 - low_x)):
            for y in range(ny):
                edge[k, y] = ref[x, y]


def side_kernel(n_x, deep, tiles, is_left, place_ref, face, halo, face_out, halo_out, edge1, edge2, edge3, onsite, onsite_out, t_out,
                pay_out, sums, t0, t1, t2, t3):
    place = place_ref[0]
    other = other_half(place)
    z = tiles * TILE
    ny = face.shape[1]
    for y in range(ny):
        for k in range(2):
            own_row = k if is_left else deep - 2 + k
            row = deep + k if is_left else k
            t0[row, y, 0:z, :] = face[own_row, y]
            t0[row, y, z : z + TILE, :] = halo[own_row, y]
        for k in range(deep):
            row = k if is_left else 2 + k
            t0[row, y, 0:z, :] = face_out[k, y]
            inner = k - 1 if is_left else k
            if 0 <= inner < deep - 1:
                t0[row, y, z : z + TILE, :] = halo_out[inner, y]
            else:
                t0[row, y, z : z + TILE, :] = jnp.zeros((TILE, LANES), jnp.float32)
        for n, (edge, ref) in enumerate(((edge1, t1), (edge2, t2), (edge3, t3))):
            for k in range(2):
                ref[(deep + n + 1 + k) if is_left else k, y] = edge[k if is_left else 2 + k, y]
    sums[...] = jnp.zeros_like(sums)
    inside, outside = (onsite, 0), (onsite_out, deep if is_left else -n_x)
    if is_left:
        zero0 = zero1 = zero2 = zero3 = deep
    else:
        zero0 = -(n_x - 2)
        zero1, zero2, zero3 = -(n_x - 3), -(n_x - 4), -(n_x - 5)
    refs = ((t0, zero0), (t1, zero1), (t2, zero2), (t3, zero3))
    for level in range(1, ITERS + 1):
        if is_left:
            lo, hi = level - deep, level
            spans = ((lo, 0, None, outside), (0, hi, sums, inside))
            out = (t_out, 0)
        else:
            lo, hi = n_x - level, n_x + deep - level
            spans = ((n_x, hi, None, outside), (lo, n_x, sums, inside))
            out = (t_out, -(n_x - deep))
        if level < ITERS:
            out = refs[level]
        prev = refs[level - 2] if level > 1 else None
        for start, stop, into, v in spans:
            if start < stop:
                sweep(level, start, stop, refs[level - 1], prev, v, out, z, into)
    pack_rows(place, other, t_out, pay_out)


def join_kernel(deep, tiles, place_ref, mid, left, right, pay_mid, pay_left, pay_right, _, whole, out, done):
    place = place_ref[0]
    other = other_half(place)
    n_x = out.shape[0]

    def join(first, count, own, pay):
        @pl.loop(0, count)
        def _(x):
            for y in range(out.shape[1]):
                for pair in range(tiles // 2):

                    def write(rows, tile, y=y):
                        out[first + x, y, rows, :] = tile

                    merge_tiles(place, other, pay, own, x, x, y, pair, pair, tiles, write)
            pltpu.make_async_copy(out.at[first + x], whole.at[first + x], done).start()

    join(deep, n_x - 2 * deep, mid, pay_mid)
    join(0, deep, left, pay_left)
    join(n_x - deep, deep, right, pay_right)
    pltpu.make_async_copy(out, whole, done).wait()


def onsite_rows(potential, place, deep):
    both = jnp.stack([potential, swap(potential)])
    n_x, _, z = potential.shape
    above = to_previous(both[..., : TILE // 2], "gz")
    below = to_next(both[..., z - TILE // 2 :], "gz")
    wide = jnp.concatenate([both, above, below], axis=3)
    before = to_next(wide[:, n_x - deep :], "gx")
    after = to_previous(wide[:, :deep], "gx")
    lane_half = (jnp.arange(LANES) >= HALF).astype(jnp.int32)
    return [jnp.where(lane_half == place, part[0][..., None], part[1][..., None]) for part in (wide, before, after)]


def by_halves(random_vectors, potential):
    n_x, ny, z, _ = random_vectors.shape
    deep = ITERS
    tiles = z // TILE
    wide = z + TILE
    place = lax.axis_index("gy").astype(jnp.int32)
    at = place[None]
    mid = n_x - 2 * deep
    pairs = tuple(range(tiles // 2))

    def packed(raw, *which):
        outs = tuple(f32(raw.shape[0], ny, TILE * len(chosen), LANES) for chosen in which)
        return call(functools.partial(pack_kernel, which, tiles), outs, n_in=1)(at, raw)

    raw_right, raw_left = random_vectors[n_x - deep :], random_vectors[:deep]
    raw_mid = random_vectors[deep : n_x - deep]
    (pay,) = packed(raw_right, pairs)
    got_right = swap(pay)
    (pay,) = packed(raw_left, pairs)
    got_left = swap(pay)
    pay, pay_rest = packed(raw_mid, pairs[:1], pairs[1:])
    got_ends = swap(pay)
    got_rest = swap(pay_rest)

    onsite, onsite_before, onsite_after = onsite_rows(potential, place, deep)

    def face(raw, got):
        outs = (f32(deep, ny, z, LANES), f32(deep, ny // 2, TILE, LANES), f32(deep, ny // 2, TILE, LANES))
        return call(functools.partial(face_kernel, tiles), outs, n_in=2)(at, raw, got)

    right, right_up, right_down = face(raw_right, got_right)
    before = to_next(right, "gx")
    left, left_up, left_down = face(raw_left, got_left)
    after = to_previous(left, "gx")

    left_down, onsite = lax.optimization_barrier((left_down, onsite))
    above = to_previous(jnp.concatenate([left_down, right_down]), "gz")
    below = to_next(jnp.concatenate([left_up, right_up]), "gz")
    halos = call(halo_kernel, f32(2 * deep, ny, TILE, LANES), n_in=2)(at, above, below)
    halo_left, halo_right = halos[:deep], halos[deep:]
    halo_before = to_next(halo_right[1:], "gx")
    halo_after = to_previous(halo_left[:-1], "gx")

    outs = (f32(mid, ny // 2, TILE, LANES), f32(mid, ny // 2, TILE, LANES))
    mid_up, mid_down = call(functools.partial(ends_kernel, tiles), outs, n_in=2)(at, raw_mid, got_ends)
    mid_above = to_previous(mid_down, "gz")
    mid_below = to_next(mid_up, "gz")

    edge = f32(4, ny, wide, LANES)
    n_sums = 2 * ITERS + 1
    sums_shape = f32(n_sums, TILE, LANES)
    deep_row = pltpu.VMEM((n_x, ny, wide, LANES), jnp.float32)
    outs = (f32(mid, ny, z, LANES), f32(mid, ny, z // 2, LANES), edge, edge, edge, sums_shape)
    t_mid, pay_mid, edge1, edge2, edge3, sums_mid = call(
        functools.partial(middle_kernel, n_x, deep, tiles), outs, [deep_row] * 4, n_in=10, limit=24
    )(at, raw_mid, got_ends, got_rest, left, right, halo_left, halo_right, mid_above, mid_below, onsite)
    back_mid = swap(pay_mid)

    side_row = pltpu.VMEM((2 * deep + 1, ny, wide, LANES), jnp.float32)
    outs = (f32(deep, ny, z, LANES), f32(deep, ny, z // 2, LANES), sums_shape)

    def side(is_left, *blocks):
        body = functools.partial(side_kernel, n_x, deep, tiles, is_left)
        return call(body, outs, [side_row] * 4, n_in=9, limit=24)(at, *blocks[:4], edge1, edge2, edge3, onsite, blocks[4])

    t_left, pay_left, sums_left = side(True, left, halo_left, before, halo_before, onsite_before)
    back_left = swap(pay_left)
    t_right, pay_right, sums_right = side(False, right, halo_right, after, halo_after, onsite_after)
    back_right = swap(pay_right)

    sums = jnp.sum(sums_mid + sums_left + sums_right, axis=1)
    sums = sums + jnp.roll(sums, HALF, axis=1)
    upper = jnp.arange(LANES) >= HALF
    sums = sum_over(jnp.where(upper, sums[ITERS:], sums[: ITERS + 1]), ("gx", "gz"))
    both = jnp.stack([sums, swap(sums)])
    turned = jnp.roll(both, HALF, axis=2)
    both = jnp.concatenate([jnp.where(upper, turned, both), jnp.where(upper, both, turned)[:, 1:]], axis=1)
    totals = jnp.where(upper.astype(jnp.int32) == place, both[0], both[1])
    moments = moments_of(totals, random_vectors.shape)

    scratch = [pltpu.VMEM((n_x, ny, z, LANES), jnp.float32), pltpu.SemaphoreType.DMA(())]
    whole = jax.ShapeDtypeStruct((n_x, ny, z, LANES), jnp.float32)
    join = call(functools.partial(join_kernel, deep, tiles), whole, scratch, n_in=7)
    return moments, join(at, t_mid, t_left, t_right, back_mid, back_left, back_right, moments)


def fits(shape):
    n_x, ny, z, lanes = shape
    return (
        lax.axis_size("gy") == 2
        and lax.axis_size("gx") > 1
        and lax.axis_size("gz") > 1
        and lanes == LANES
        and n_x > 2 * ITERS
        and ny % 2 == 0
        and z % (2 * TILE) == 0
        and z >= 4 * TILE
        and ITERS == TILE // 2
    )


def shards(random_vectors, potential):
    if fits(random_vectors.shape):
        return by_halves(random_vectors, potential)
    return step_by_step(random_vectors, potential)


def solution(mesh):
    in_specs = (P("gx", "gy", "gz", None), P("gx", "gy", "gz"))
    out_specs = (P(), P("gx", "gy", "gz", None))
    return jax.shard_map(shards, mesh=mesh, in_specs=in_specs, out_specs=out_specs, check_vma=False)
```

time: 99.6 us -> 106 us (1.064)
  Pallas kernels: 0 us -> 14.9 us
  waiting for transfers between devices: 36.8 us -> 48.6 us
  local copies, waits for them, and re-layouts: 11.1 us -> 1.69 us
  other arithmetic: 11.8 us -> 2.85 us
  blocking collectives: 13.9 us -> 12.2 us
    pallas_call x0 -> x11, Pallas kernels: none -> 14.9 us  [held(): run(place, *(pltpu.with_memory_space_constraint(block, pltpu.VMEM) for bl...]
    ppermute x20 -> x21, waiting for transfers between devices: 36.8 us -> 48.6 us  [the longest x9 26.4 us: swap(): return lax.ppermute(block, 'gy', [(0, 1), (1, 0)])]
    slice x29 -> x6, local copies, waits for them, and re-layouts: 10.5 us -> 1.65 us  [the longest x1 1.43 us: by_halves(): raw_right, raw_left = (random_vectors[n_x - deep:], random_vectors[:deep])]
    sub x3 -> x0, other arithmetic: 4.72 us -> none  [the longest x2 4.71 us: shards(): terms.append(2.0 * apply_hamiltonian(terms[-1]) - terms[-2])]
    reduce_sum x2, other arithmetic: 4.08 us -> 0.04 us  [the longest x1 0.02 us: sum_over(): return jnp.sum(lax.all_to_all(copies, axes, 0, 0), axis=0)]
    div x2 -> x1, other arithmetic: 2.82 us -> 0.08 us  [moments_of(): return jnp.where(first, totals, 2.0 * totals - lower) / sites]
    select_n x0 -> x6, other arithmetic: none -> 2.32 us  [the longest x2 2.14 us: onsite_rows(): jnp.where(lane_half == place, part[0][..., None], part[1][..., None])]
    all_to_all x1, blocking collectives: 13.9 us -> 12.2 us  [sum_over(): return jnp.sum(lax.all_to_all(copies, axes, 0, 0), axis=0)]
  transfers between devices with their start and end apart: 20 -> 21, of which waited for: 4 -> 10; matrix products, arithmetic and copies ran while one was open for 6% -> 3% of each run, Pallas kernels for 0% -> 10%
where the time goes in v2:
time: 106 us
  waiting for transfers between devices  48.6 us (46%)
  starting transfers between devices  24.8 us (23%)
  Pallas kernels  14.9 us (14%)
  blocking collectives  12.2 us (12%)
  other arithmetic  2.85 us (3%)
  local copies, waits for them, and re-layouts  1.69 us (2%)
    ppermute x9, waiting for transfers between devices, swap(): return lax.ppermute(block, 'gy', [(0, 1), (1, 0)])  26.4 us
    ppermute x6, waiting for transfers between devices, to_next(): lax.ppermute(block, axis, [(i, (i + 1) % count) for i in range(count)])  18.3 us
    pallas_call x11, Pallas kernels, held(): run(place, *(pltpu.with_memory_space_constraint(block, pltpu.VMEM) for bl...  14.9 us
    all_to_all x1, blocking collectives, sum_over(): return jnp.sum(lax.all_to_all(copies, axes, 0, 0), axis=0)  12.2 us
    ppermute x9, starting transfers between devices, swap(): return lax.ppermute(block, 'gy', [(0, 1), (1, 0)])  11.8 us
    ppermute x6, starting transfers between devices, to_previous(): lax.ppermute(block, axis, [((i + 1) % count, i) for i in range(count)])  9.39 us
    ppermute x6, waiting for transfers between devices, to_previous(): lax.ppermute(block, axis, [((i + 1) % count, i) for i in range(count)])  3.91 us
    ppermute x6, starting transfers between devices, to_next(): lax.ppermute(block, axis, [(i, (i + 1) % count) for i in range(count)])  3.54 us
  transfers between devices with their start and end apart: 21, of which 10 were waited for; matrix products, arithmetic and copies ran while one was open for 3% of the time, Pallas kernels for 10%

profile of v2, /device:TPU:0, one launch (start us, length us, event | category | flops | bytes accessed | tf_op | source)
XLA Modules:
  0.0 105.8 jit_solution(17816973532996193916)
XLA Ops:
  0.7 1.4 %fusion.11 = (f32[4,8,32,128]{3,2,1,0:T(8,128)S(1)}, f32[4,8,32,128]{3,2,1,0:T(8,128)S(1)}) fusion(f32[16,8,32,128]{3,2,1,0:T(8,128)} %param.2), kind=kLoop, calls=%fused_computation.47 | loop fusion | bytes 2097152 | tf_op jit(solution)/shard_map/slice | solution.py:421
  2.4 3.1 %collective-permute-start.2 = (f32[4,8,16,128]{3,2,1,0:T(8,128)S(1)}, f32[4,8,16,128]{3,2,1,0:T(8,128)S(1)}, u32[]{:S(2)}, u32[]{:S(2)}) collective-permute-start(f32[4,8,16,128]{3,2,1,0:T(8,128)S(1)} %shard_map.42), channel_id=1, source_target_pairs={{0,4},{4,0},{1,5},{5,1},{2,6},{6,2},{3,7},{7,3},{8,12},{12,8},{9,1... | collective-permute-start | bytes 786440 | tf_op jit(solution)/shard_map/ppermute | solution.py:49
  5.9 2.0 %collective-permute-start.3 = (f32[4,8,16,128]{3,2,1,0:T(8,128)S(1)}, f32[4,8,16,128]{3,2,1,0:T(8,128)S(1)}, u32[]{:S(2)}, u32[]{:S(2)}) collective-permute-start(f32[4,8,16,128]{3,2,1,0:T(8,128)S(1)} %shard_map.44), channel_id=1, source_target_pairs={{0,4},{4,0},{1,5},{5,1},{2,6},{6,2},{3,7},{7,3},{8,12},{12,8},{9,1... | collective-permute-start | bytes 786440 | tf_op jit(solution)/shard_map/ppermute | solution.py:49
  8.1 0.7 shard_map.41
  8.9 5.2 %collective-permute-done.4 = f32[16,8,32]{2,1,0:T(8,128)S(1)} collective-permute-done((f32[16,8,32]{2,1,0:T(8,128)S(1)}, f32[16,8,32]{2,1,0:T(8,128)S(1)}, u32[]{:S(2)}, u32[]{:S(2)}) %collective-permute-start.4) | collective-permute-done | bytes 16416 | tf_op jit(solution)/shard_map/ppermute | solution.py:49
  14.7 2.0 %collective-permute-done.5 = f32[2,16,8,4]{3,2,1,0:T(8,128)S(1)} collective-permute-done((f32[2,16,8,4]{3,2,1,0:T(8,128)S(1)}, f32[2,16,8,4]{3,2,1,0:T(8,128)S(1)}, u32[]{:S(2)}, u32[]{:S(2)}) %collective-permute-start.5) | collective-permute-done | bytes 4128 | tf_op jit(solution)/shard_map/ppermute | solution.py:45
  16.7 2.4 %collective-permute-start.1 = (f32[8,8,8,128]{3,2,1,0:T(8,128)S(1)}, f32[8,8,8,128]{3,2,1,0:T(8,128)S(1)}, u32[]{:S(2)}, u32[]{:S(2)}) collective-permute-start(f32[8,8,8,128]{3,2,1,0:T(8,128)S(1)} %get-tuple-element.27), channel_id=1, source_target_pairs={{0,4},{4,0},{1,5},{5,1},{2,6},{6,2},{3,7},{7,3},{8,12},{12,8},{9,1... | collective-permute-start | bytes 786440 | tf_op jit(solution)/shard_map/ppermute | solution.py:49
  19.2 1.0 collective-permute-done.6
  20.4 2.0 %collective-permute-start.13 = (f32[2,4,8,40]{3,2,1,0:T(8,128)S(1)}, f32[2,4,8,40]{3,2,1,0:T(8,128)S(1)}, u32[]{:S(2)}, u32[]{:S(2)}) collective-permute-start(f32[2,4,8,40]{3,2,1,0:T(8,128)S(1)} %get-tuple-element.56), channel_id=1, source_target_pairs={{0,8},{8,16},{16,24},{24,0},{1,9},{9,17},{17,25},{25,1},{2,10},{10... | collective-permute-start | bytes 30728 | tf_op jit(solution)/shard_map/ppermute | solution.py:40
  22.4 1.4 %broadcast_select_fusion.onsite = f32[16,8,40,128]{3,2,1,0:T(8,128)S(1)} fusion(f32[16,8,40]{2,1,0:T(8,128)S(1)} %get-tuple-element.59, f32[16,8,40]{2,1,0:T(8,128)S(1)} %get-tuple-element.58, pred[128]{0:T(512)(128)(4,1)S(1)} %convert_compare_fusion), kind=kLoop, calls=%fused_computation | loop fusion | flops 655360 | bytes 2662528 | tf_op jit(solution)/shard_map/jit(_where)/select_n | solution.py:404
  23.8 2.5 %collective-permute-done.13 = f32[2,4,8,40]{3,2,1,0:T(8,128)S(1)} collective-permute-done((f32[2,4,8,40]{3,2,1,0:T(8,128)S(1)}, f32[2,4,8,40]{3,2,1,0:T(8,128)S(1)}, u32[]{:S(2)}, u32[]{:S(2)}) %collective-permute-start.13) | collective-permute-done | bytes 10272 | tf_op jit(solution)/shard_map/ppermute | solution.py:40
  26.3 2.0 %collective-permute-start.16 = (f32[2,4,8,40]{3,2,1,0:T(8,128)S(1)}, f32[2,4,8,40]{3,2,1,0:T(8,128)S(1)}, u32[]{:S(2)}, u32[]{:S(2)}) collective-permute-start(f32[2,4,8,40]{3,2,1,0:T(8,128)S(1)} %get-tuple-element.57), channel_id=1, source_target_pairs={{8,0},{16,8},{24,16},{0,24},{9,1},{17,9},{25,17},{1,25},{10,2},{18... | collective-permute-start | bytes 30728 | tf_op jit(solution)/shard_map/ppermute | solution.py:45
  28.3 1.9 %collective-permute-done.16 = f32[2,4,8,40]{3,2,1,0:T(8,128)S(1)} collective-permute-done((f32[2,4,8,40]{3,2,1,0:T(8,128)S(1)}, f32[2,4,8,40]{3,2,1,0:T(8,128)S(1)}, u32[]{:S(2)}, u32[]{:S(2)}) %collective-permute-start.16) | collective-permute-done | bytes 10272 | tf_op jit(solution)/shard_map/ppermute | solution.py:45
  31.6 3.8 %collective-permute-start.14 = (f32[4,8,32,128]{3,2,1,0:T(8,128)S(1)}, f32[4,8,32,128]{3,2,1,0:T(8,128)S(1)}, u32[]{:S(2)}, u32[]{:S(2)}) collective-permute-start(f32[4,8,32,128]{3,2,1,0:T(8,128)S(1)} %get-tuple-element.28.left.face), channel_id=1, source_target_pairs={{8,0},{16,8},{24,16},{0,24},{9,1},{17,9},{25,17},{1,25},{10,2},{18... | collective-permute-start | bytes 1572872 | tf_op jit(solution)/shard_map/ppermute | solution.py:45
  35.5 0.7 broadcast_select_fusion.2
  36.2 0.6 shard_map.47
  37.3 1.4 %collective-permute-start.9 = (f32[8,4,8,128]{3,2,1,0:T(8,128)S(1)}, f32[8,4,8,128]{3,2,1,0:T(8,128)S(1)}, u32[]{:S(2)}, u32[]{:S(2)}) collective-permute-start(f32[8,4,8,128]{3,2,1,0:T(8,128)S(1)} %get-tuple-element.35), channel_id=1, source_target_pairs={{1,0},{2,1},{3,2},{0,3},{5,4},{6,5},{7,6},{4,7},{9,8},{10,9},{11,1... | collective-permute-start | bytes 393224 | tf_op jit(solution)/shard_map/ppermute | solution.py:45
  38.8 2.5 %collective-permute-done.10.below = f32[8,4,8,128]{3,2,1,0:T(8,128)S(1)} collective-permute-done((f32[8,4,8,128]{3,2,1,0:T(8,128)S(1)}, f32[8,4,8,128]{3,2,1,0:T(8,128)S(1)}, u32[]{:S(2)}, u32[]{:S(2)}) %collective-permute-start.10) | collective-permute-done | bytes 131104 | tf_op jit(solution)/shard_map/ppermute | solution.py:40
  41.3 2.1 %collective-permute-start.15 = (f32[3,8,8,128]{3,2,1,0:T(8,128)S(1)}, f32[3,8,8,128]{3,2,1,0:T(8,128)S(1)}, u32[]{:S(2)}, u32[]{:S(2)}) collective-permute-start(f32[3,8,8,128]{3,2,1,0:T(8,128)S(1)} %get-tuple-element.53), channel_id=1, source_target_pairs={{8,0},{16,8},{24,16},{0,24},{9,1},{17,9},{25,17},{1,25},{10,2},{18... | collective-permute-start | bytes 294920 | tf_op jit(solution)/shard_map/ppermute | solution.py:45
  43.4 6.0 %shard_map.48 = (f32[8,8,32,128]{3,2,1,0:T(8,128)S(1)}, f32[8,8,16,128]{3,2,1,0:T(8,128)S(1)}, f32[4,8,40,128]{3,2,1,0:T(8,128)S(1)}, f32[4,8,40,128]{3,2,1,0:T(...) custom-call(s32[1]{0:T(128)} %bitcast.place_ref, f32[8,8,32,128]{3,2,1,0:T(8,128)S(1)} %slice.90.src.own, ...), custom_call_target="tpu_custom_call" | custom-call | tf_op jit(solution)/shard_map/pallas_call | solution.py:102
  49.5 12.2 %collective-permute-done.12.halo_out = f32[3,8,8,128]{3,2,1,0:T(8,128)S(1)} collective-permute-done((f32[3,8,8,128]{3,2,1,0:T(8,128)S(1)}, f32[3,8,8,128]{3,2,1,0:T(8,128)S(1)}, u32[]{:S(2)}, u32[]{:S(2)}) %collective-permute-start.12) | collective-permute-done | bytes 98336 | tf_op jit(solution)/shard_map/ppermute | solution.py:40
  61.7 2.0 %shard_map.49 = (f32[4,8,32,128]{3,2,1,0:T(8,128)S(1)}, f32[4,8,16,128]{3,2,1,0:T(8,128)S(1)}, f32[9,8,128]{2,1,0:T(8,128)S(1)}) custom-call(s32[1]{0:T(128)} %bitcast.place_ref, f32[4,8,32,128]{3,2,1,0:T(8,128)S(1)} %get-tuple-element.28.left.face, f32[4,8,8,128]{3,2,1,0:T(8,128)S(1)} %get-tuple-element.54.halo_left.halo, ...), custom_call_target="tpu_custom_call" | custom-call | tf_op jit(solution)/shard_map/pallas_call | solution.py:102
  63.7 2.0 %shard_map.50 = (f32[4,8,32,128]{3,2,1,0:T(8,128)S(1)}, f32[4,8,16,128]{3,2,1,0:T(8,128)S(1)}, f32[9,8,128]{2,1,0:T(8,128)S(1)}) custom-call(s32[1]{0:T(128)} %bitcast.place_ref, f32[4,8,32,128]{3,2,1,0:T(8,128)S(1)} %get-tuple-element.29.right.face, f32[4,8,8,128]{3,2,1,0:T(8,128)S(1)} %get-tuple-element.55.halo_right.halo, ...), custom_call_target="tpu_custom_call" | custom-call | tf_op jit(solution)/shard_map/pallas_call | solution.py:102
  65.9 12.2 %all_to_all.5 = f32[16,5,128]{2,1,0:T(8,128)S(1)} all-to-all(f32[16,5,128]{2,1,0:T(8,128)S(1)} %broadcast_in_dim.132), channel_id=1, replica_groups=mesh['gx'=4,'gy'=2,'gz'=4] {'gx','gz'}, dimensions={0} | all-to-all | bytes 81920 | tf_op jit(solution)/shard_map/all_to_all | solution.py:57
  78.1 1.3 %collective-permute-start.17 = (f32[5,128]{1,0:T(8,128)S(1)}, f32[5,128]{1,0:T(8,128)S(1)}, u32[]{:S(2)}, u32[]{:S(2)}) collective-permute-start(f32[5,128]{1,0:T(8,128)S(1)} %reduce_sum.19), channel_id=1, source_target_pairs={{0,4},{4,0},{1,5},{5,1},{2,6},{6,2},{3,7},{7,3},{8,12},{12,8},{9,1... | collective-permute-start | bytes 7688 | tf_op jit(solution)/shard_map/ppermute | solution.py:49
  79.4 0.8 collective-permute-start.18
  80.2 1.2 %collective-permute-start.19 = (f32[4,8,16,128]{3,2,1,0:T(8,128)S(1)}, f32[4,8,16,128]{3,2,1,0:T(8,128)S(1)}, u32[]{:S(2)}, u32[]{:S(2)}) collective-permute-start(f32[4,8,16,128]{3,2,1,0:T(8,128)S(1)} %get-tuple-element.48), channel_id=1, source_target_pairs={{0,4},{4,0},{1,5},{5,1},{2,6},{6,2},{3,7},{7,3},{8,12},{12,8},{9,1... | collective-permute-start | bytes 786440 | tf_op jit(solution)/shard_map/ppermute | solution.py:49
  81.4 0.8 collective-permute-start.20
  82.6 11.6 %collective-permute-done.18.pay_mid = f32[8,8,16,128]{3,2,1,0:T(8,128)S(1)} collective-permute-done((f32[8,8,16,128]{3,2,1,0:T(8,128)S(1)}, f32[8,8,16,128]{3,2,1,0:T(8,128)S(1)}, u32[]{:S(2)}, u32[]{:S(2)}) %collective-permute-start.18) | collective-permute-done | bytes 524320 | tf_op jit(solution)/shard_map/ppermute | solution.py:49
  94.2 5.6 %collective-permute-done.19.pay_left = f32[4,8,16,128]{3,2,1,0:T(8,128)S(1)} collective-permute-done((f32[4,8,16,128]{3,2,1,0:T(8,128)S(1)}, f32[4,8,16,128]{3,2,1,0:T(8,128)S(1)}, u32[]{:S(2)}, u32[]{:S(2)}) %collective-permute-start.19) | collective-permute-done | bytes 262176 | tf_op jit(solution)/shard_map/ppermute | solution.py:49
  99.8 4.0 %collective-permute-done.20.pay_right = f32[4,8,16,128]{3,2,1,0:T(8,128)S(1)} collective-permute-done((f32[4,8,16,128]{3,2,1,0:T(8,128)S(1)}, f32[4,8,16,128]{3,2,1,0:T(8,128)S(1)}, u32[]{:S(2)}, u32[]{:S(2)}) %collective-permute-start.20) | collective-permute-done | bytes 262176 | tf_op jit(solution)/shard_map/ppermute | solution.py:49
  103.8 2.1 %shard_map.51 = f32[16,8,32,128]{3,2,1,0:T(8,128)} custom-call(s32[1]{0:T(128)} %bitcast.place_ref, f32[8,8,32,128]{3,2,1,0:T(8,128)S(1)} %get-tuple-element.44.mid, f32[4,8,32,128]{3,2,1,0:T(8,128)S(1)} %get-tuple-element.45.left, f32[4,8,32,128]{3,2,1,0:T(8,128)S(1)} %get-tuple-element.46.right, f32[8,8,16,128]{3,2,1,0:T(8,128)S(1)} %collective-permute-done.18.pay_mid, ...), custom_call_target="tpu_custom_call" | custom-call | tf_op jit(solution)/shard_map/pallas_call | solution.py:102
  (57 shorter events, 4.4 us)
Async XLA Ops:
  0.6 7.3 %copy-start.1 = (f32[16,8,32,128]{3,2,1,0:T(8,128)S(1)}, f32[16,8,32,128]{3,2,1,0:T(8,128)}, u32[]{:S(2)}) copy-start(f32[16,8,32,128]{3,2,1,0:T(8,128)} %param.2) | copy-start | bytes 6291460
  0.6 4.9 %copy-start.2 = (f32[16,8,32]{2,1,0:T(8,128)S(1)}, f32[16,8,32]{2,1,0:T(8,128)}, u32[]{:S(2)}) copy-start(f32[16,8,32]{2,1,0:T(8,128)} %param.3) | copy-start | bytes 49156
  2.4 27.8 %collective-permute-start.2 = (f32[4,8,16,128]{3,2,1,0:T(8,128)S(1)}, f32[4,8,16,128]{3,2,1,0:T(8,128)S(1)}, u32[]{:S(2)}, u32[]{:S(2)}) collective-permute-start(f32[4,8,16,128]{3,2,1,0:T(8,128)S(1)} %shard_map.42), channel_id=1, source_target_pairs={{0,4},{4,0},{1,5},{5,1},{2,6},{6,2},{3,7},{7,3},{8,12},{12,8},{9,1... | collective-permute-start | bytes 786440 | tf_op jit(solution)/shard_map/ppermute | solution.py:49
  5.5 8.6 %collective-permute-start.4 = (f32[16,8,32]{2,1,0:T(8,128)S(1)}, f32[16,8,32]{2,1,0:T(8,128)S(1)}, u32[]{:S(2)}, u32[]{:S(2)}) collective-permute-start(f32[16,8,32]{2,1,0:T(8,128)S(1)} %copy-done.2), channel_id=1, source_target_pairs={{0,4},{4,0},{1,5},{5,1},{2,6},{6,2},{3,7},{7,3},{8,12},{12,8},{9,1... | collective-permute-start | bytes 49160 | tf_op jit(solution)/shard_map/ppermute | solution.py:49
  5.9 24.7 %collective-permute-start.3 = (f32[4,8,16,128]{3,2,1,0:T(8,128)S(1)}, f32[4,8,16,128]{3,2,1,0:T(8,128)S(1)}, u32[]{:S(2)}, u32[]{:S(2)}) collective-permute-start(f32[4,8,16,128]{3,2,1,0:T(8,128)S(1)} %shard_map.44), channel_id=1, source_target_pairs={{0,4},{4,0},{1,5},{5,1},{2,6},{6,2},{3,7},{7,3},{8,12},{12,8},{9,1... | collective-permute-start | bytes 786440 | tf_op jit(solution)/shard_map/ppermute | solution.py:49
  8.7 22.9 %collective-permute-start = (f32[8,8,8,128]{3,2,1,0:T(8,128)S(1)}, f32[8,8,8,128]{3,2,1,0:T(8,128)S(1)}, u32[]{:S(2)}, u32[]{:S(2)}) collective-permute-start(f32[8,8,8,128]{3,2,1,0:T(8,128)S(1)} %get-tuple-element.26), channel_id=1, source_target_pairs={{0,4},{4,0},{1,5},{5,1},{2,6},{6,2},{3,7},{7,3},{8,12},{12,8},{9,1... | collective-permute-start | bytes 786440 | tf_op jit(solution)/shard_map/ppermute | solution.py:49
  14.2 2.6 %collective-permute-start.5 = (f32[2,16,8,4]{3,2,1,0:T(8,128)S(1)}, f32[2,16,8,4]{3,2,1,0:T(8,128)S(1)}, u32[]{:S(2)}, u32[]{:S(2)}) collective-permute-start(f32[2,16,8,4]{3,2,1,0:T(8,128)S(1)} %get-tuple-element.60), channel_id=1, source_target_pairs={{1,0},{2,1},{3,2},{0,3},{5,4},{6,5},{7,6},{4,7},{9,8},{10,9},{11,1... | collective-permute-start | bytes 12296 | tf_op jit(solution)/shard_map/ppermute | solution.py:45
  14.2 6.0 %collective-permute-start.6 = (f32[2,16,8,4]{3,2,1,0:T(8,128)S(1)}, f32[2,16,8,4]{3,2,1,0:T(8,128)S(1)}, u32[]{:S(2)}, u32[]{:S(2)}) collective-permute-start(f32[2,16,8,4]{3,2,1,0:T(8,128)S(1)} %get-tuple-element.61), channel_id=1, source_target_pairs={{0,1},{1,2},{2,3},{3,0},{4,5},{5,6},{6,7},{7,4},{8,9},{9,10},{10,1... | collective-permute-start | bytes 12296 | tf_op jit(solution)/shard_map/ppermute | solution.py:40
  16.7 22.0 %collective-permute-start.1 = (f32[8,8,8,128]{3,2,1,0:T(8,128)S(1)}, f32[8,8,8,128]{3,2,1,0:T(8,128)S(1)}, u32[]{:S(2)}, u32[]{:S(2)}) collective-permute-start(f32[8,8,8,128]{3,2,1,0:T(8,128)S(1)} %get-tuple-element.27), channel_id=1, source_target_pairs={{0,4},{4,0},{1,5},{5,1},{2,6},{6,2},{3,7},{7,3},{8,12},{12,8},{9,1... | collective-permute-start | bytes 786440 | tf_op jit(solution)/shard_map/ppermute | solution.py:49
  20.4 5.9 %collective-permute-start.13 = (f32[2,4,8,40]{3,2,1,0:T(8,128)S(1)}, f32[2,4,8,40]{3,2,1,0:T(8,128)S(1)}, u32[]{:S(2)}, u32[]{:S(2)}) collective-permute-start(f32[2,4,8,40]{3,2,1,0:T(8,128)S(1)} %get-tuple-element.56), channel_id=1, source_target_pairs={{0,8},{8,16},{16,24},{24,0},{1,9},{9,17},{17,25},{25,1},{2,10},{10... | collective-permute-start | bytes 30728 | tf_op jit(solution)/shard_map/ppermute | solution.py:40
  26.3 3.9 %collective-permute-start.16 = (f32[2,4,8,40]{3,2,1,0:T(8,128)S(1)}, f32[2,4,8,40]{3,2,1,0:T(8,128)S(1)}, u32[]{:S(2)}, u32[]{:S(2)}) collective-permute-start(f32[2,4,8,40]{3,2,1,0:T(8,128)S(1)} %get-tuple-element.57), channel_id=1, source_target_pairs={{8,0},{16,8},{24,16},{0,24},{9,1},{17,9},{25,17},{1,25},{10,2},{18... | collective-permute-start | bytes 30728 | tf_op jit(solution)/shard_map/ppermute | solution.py:45
  31.0 5.8 %collective-permute-start.7 = (f32[8,4,8,128]{3,2,1,0:T(8,128)S(1)}, f32[8,4,8,128]{3,2,1,0:T(8,128)S(1)}, u32[]{:S(2)}, u32[]{:S(2)}) collective-permute-start(f32[8,4,8,128]{3,2,1,0:T(8,128)S(1)} %pad_maximum_fusion.2), channel_id=1, source_target_pairs={{1,0},{2,1},{3,2},{0,3},{5,4},{6,5},{7,6},{4,7},{9,8},{10,9},{11,1... | collective-permute-start | bytes 393224 | tf_op jit(solution)/shard_map/ppermute | solution.py:45
  31.1 6.2 %collective-permute-start.8 = (f32[8,4,8,128]{3,2,1,0:T(8,128)S(1)}, f32[8,4,8,128]{3,2,1,0:T(8,128)S(1)}, u32[]{:S(2)}, u32[]{:S(2)}) collective-permute-start(f32[8,4,8,128]{3,2,1,0:T(8,128)S(1)} %pad_maximum_fusion.3), channel_id=1, source_target_pairs={{0,1},{1,2},{2,3},{3,0},{4,5},{5,6},{6,7},{7,4},{8,9},{9,10},{10,1... | collective-permute-start | bytes 393224 | tf_op jit(solution)/shard_map/ppermute | solution.py:40
  31.6 30.1 %collective-permute-start.11 = (f32[4,8,32,128]{3,2,1,0:T(8,128)S(1)}, f32[4,8,32,128]{3,2,1,0:T(8,128)S(1)}, u32[]{:S(2)}, u32[]{:S(2)}) collective-permute-start(f32[4,8,32,128]{3,2,1,0:T(8,128)S(1)} %get-tuple-element.29.right.face), channel_id=1, source_target_pairs={{0,8},{8,16},{16,24},{24,0},{1,9},{9,17},{17,25},{25,1},{2,10},{10... | collective-permute-start | bytes 1572872 | tf_op jit(solution)/shard_map/ppermute | solution.py:40
  31.6 32.1 %collective-permute-start.14 = (f32[4,8,32,128]{3,2,1,0:T(8,128)S(1)}, f32[4,8,32,128]{3,2,1,0:T(8,128)S(1)}, u32[]{:S(2)}, u32[]{:S(2)}) collective-permute-start(f32[4,8,32,128]{3,2,1,0:T(8,128)S(1)} %get-tuple-element.28.left.face), channel_id=1, source_target_pairs={{8,0},{16,8},{24,16},{0,24},{9,1},{17,9},{25,17},{1,25},{10,2},{18... | collective-permute-start | bytes 1572872 | tf_op jit(solution)/shard_map/ppermute | solution.py:45
  36.9 4.4 %collective-permute-start.10 = (f32[8,4,8,128]{3,2,1,0:T(8,128)S(1)}, f32[8,4,8,128]{3,2,1,0:T(8,128)S(1)}, u32[]{:S(2)}, u32[]{:S(2)}) collective-permute-start(f32[8,4,8,128]{3,2,1,0:T(8,128)S(1)} %get-tuple-element.36), channel_id=1, source_target_pairs={{0,1},{1,2},{2,3},{3,0},{4,5},{5,6},{6,7},{7,4},{8,9},{9,10},{10,1... | collective-permute-start | bytes 393224 | tf_op jit(solution)/shard_map/ppermute | solution.py:40
  37.3 6.1 %collective-permute-start.9 = (f32[8,4,8,128]{3,2,1,0:T(8,128)S(1)}, f32[8,4,8,128]{3,2,1,0:T(8,128)S(1)}, u32[]{:S(2)}, u32[]{:S(2)}) collective-permute-start(f32[8,4,8,128]{3,2,1,0:T(8,128)S(1)} %get-tuple-element.35), channel_id=1, source_target_pairs={{1,0},{2,1},{3,2},{0,3},{5,4},{6,5},{7,6},{4,7},{9,8},{10,9},{11,1... | collective-permute-start | bytes 393224 | tf_op jit(solution)/shard_map/ppermute | solution.py:45
  38.7 22.9 %collective-permute-start.12 = (f32[3,8,8,128]{3,2,1,0:T(8,128)S(1)}, f32[3,8,8,128]{3,2,1,0:T(8,128)S(1)}, u32[]{:S(2)}, u32[]{:S(2)}) collective-permute-start(f32[3,8,8,128]{3,2,1,0:T(8,128)S(1)} %get-tuple-element.52), channel_id=1, source_target_pairs={{0,8},{8,16},{16,24},{24,0},{1,9},{9,17},{17,25},{25,1},{2,10},{10... | collective-permute-start | bytes 294920 | tf_op jit(solution)/shard_map/ppermute | solution.py:40
  41.3 22.4 %collective-permute-start.15 = (f32[3,8,8,128]{3,2,1,0:T(8,128)S(1)}, f32[3,8,8,128]{3,2,1,0:T(8,128)S(1)}, u32[]{:S(2)}, u32[]{:S(2)}) collective-permute-start(f32[3,8,8,128]{3,2,1,0:T(8,128)S(1)} %get-tuple-element.53), channel_id=1, source_target_pairs={{8,0},{16,8},{24,16},{0,24},{9,1},{17,9},{25,17},{1,25},{10,2},{18... | collective-permute-start | bytes 294920 | tf_op jit(solution)/shard_map/ppermute | solution.py:45
  78.1 4.1 %collective-permute-start.17 = (f32[5,128]{1,0:T(8,128)S(1)}, f32[5,128]{1,0:T(8,128)S(1)}, u32[]{:S(2)}, u32[]{:S(2)}) collective-permute-start(f32[5,128]{1,0:T(8,128)S(1)} %reduce_sum.19), channel_id=1, source_target_pairs={{0,4},{4,0},{1,5},{5,1},{2,6},{6,2},{3,7},{7,3},{8,12},{12,8},{9,1... | collective-permute-start | bytes 7688 | tf_op jit(solution)/shard_map/ppermute | solution.py:49
  79.4 14.8 %collective-permute-start.18 = (f32[8,8,16,128]{3,2,1,0:T(8,128)S(1)}, f32[8,8,16,128]{3,2,1,0:T(8,128)S(1)}, u32[]{:S(2)}, u32[]{:S(2)}) collective-permute-start(f32[8,8,16,128]{3,2,1,0:T(8,128)S(1)} %get-tuple-element.47), channel_id=1, source_target_pairs={{0,4},{4,0},{1,5},{5,1},{2,6},{6,2},{3,7},{7,3},{8,12},{12,8},{9,1... | collective-permute-start | bytes 1572872 | tf_op jit(solution)/shard_map/ppermute | solution.py:49
  80.2 19.6 %collective-permute-start.19 = (f32[4,8,16,128]{3,2,1,0:T(8,128)S(1)}, f32[4,8,16,128]{3,2,1,0:T(8,128)S(1)}, u32[]{:S(2)}, u32[]{:S(2)}) collective-permute-start(f32[4,8,16,128]{3,2,1,0:T(8,128)S(1)} %get-tuple-element.48), channel_id=1, source_target_pairs={{0,4},{4,0},{1,5},{5,1},{2,6},{6,2},{3,7},{7,3},{8,12},{12,8},{9,1... | collective-permute-start | bytes 786440 | tf_op jit(solution)/shard_map/ppermute | solution.py:49
  81.4 22.4 %collective-permute-start.20 = (f32[4,8,16,128]{3,2,1,0:T(8,128)S(1)}, f32[4,8,16,128]{3,2,1,0:T(8,128)S(1)}, u32[]{:S(2)}, u32[]{:S(2)}) collective-permute-start(f32[4,8,16,128]{3,2,1,0:T(8,128)S(1)} %get-tuple-element.49), channel_id=1, source_target_pairs={{0,4},{4,0},{1,5},{5,1},{2,6},{6,2},{3,7},{7,3},{8,12},{12,8},{9,1... | collective-permute-start | bytes 786440 | tf_op jit(solution)/shard_map/ppermute | solution.py:49
  82.6 23.3 %copy-start = (f32[9,128]{1,0:T(8,128)}, f32[9,128]{1,0:T(8,128)S(1)}, u32[]{:S(2)}) copy-start(f32[9,128]{1,0:T(8,128)S(1)} %select_multiply_fusion._) | copy-start | bytes 13828
